TPU v7x, 32 devices: a whole 2x2x4 slice. The times are simulated.
32 devices in a mesh: tile: 8 (over y, x, core), aux: 4 (over z).
Axes of the slice: x: 2, y: 2, z: 4, core: 2. Of those that a mesh axis runs over, the one named last changes fastest.
Arguments:
- amps: bfloat16 [8, 8, 128, 128], P('tile'), may hold values from -6 to 6
- fitted: bfloat16 [2048, 8, 128], P('aux'), may hold values from -0.375 to 0.375
- screen: int32 [16, 8], P('aux'), may hold values 0 or 1
- owner: int32 [8], replicated, may hold values from 0 to 7, each once
- eps_occ: float32 [8], replicated, may hold values from -2 to -0.5
- eps_vir: float32 [128], replicated, may hold values from 0.5 to 2
Outputs:
- update: bfloat16 [8, 128, 8, 128], P(None, None, 'tile')
Inputs may be any that keep to these rules, and one draw needn't show every extreme that they name: owner is a permutation of the occupied orbitals.
All inputs are finite; a program needn't handle non-finite values. No bound on the sum of `screen` on one device may be relied on, other than what follows from the above.
Results may differ from a plain program's by a relative error of at most 0.0034.
Values may be sent and summed in bfloat16 or wider, within the bound.
No kernel may reach another device: no remote copies, remote signals or barrier semaphores. Data moves between devices by JAX's collectives and lax.ppermute only.
A program may use at most 64 MiB of HBM per device.

v0:
```python
import jax
import jax.numpy as jnp
from jax import lax
from jax.sharding import PartitionSpec as P


def on_device(amps, fitted, screen, owner, eps_occ, eps_vir):
    occ_dev = amps.shape[0]
    qblock_size = fitted.shape[0] // screen.shape[0]
    tile_mask = jnp.repeat(screen, qblock_size, axis=0).astype(jnp.bfloat16)
    screened = fitted * tile_mask[:, :, None]
    permuted = jnp.take(amps, owner, axis=1)
    received = lax.all_to_all(permuted, "tile", split_axis=1, concat_axis=0, tiled=True)
    intermed = jnp.einsum(
        "qkc,kpcb->qpb", screened, received, preferred_element_type=jnp.float32
    ).astype(jnp.bfloat16)
    partial_cycle = jnp.einsum(
        "qia,qpb->iapb", screened, intermed, preferred_element_type=jnp.float32
    )
    slot_start = lax.axis_index("tile") * occ_dev
    own_owner = lax.dynamic_slice_in_dim(owner, slot_start, occ_dev, 0)
    eps_slot = jnp.take(eps_occ, own_owner, axis=0)
    virt_pair = (
        eps_vir[None, :, None, None] + eps_vir[None, None, None, :] - eps_slot[None, None, :, None]
    )
    occ_rows = partial_cycle.shape[0]
    aux_count = lax.axis_size("aux")
    share_rows = -(-occ_rows // aux_count)
    extra_rows = share_rows * aux_count - occ_rows
    padded = jnp.pad(partial_cycle, ((0, extra_rows), (0, 0), (0, 0), (0, 0)))
    cycle_share = lax.psum_scatter(padded, "aux", scatter_dimension=0, tiled=True)
    eps_padded = jnp.pad(eps_occ, (0, extra_rows))
    eps_share = lax.dynamic_slice_in_dim(
        eps_padded, lax.axis_index("aux") * share_rows, share_rows, 0
    )
    denominator = virt_pair - eps_share[:, None, None, None]
    divided = (cycle_share / denominator).astype(jnp.bfloat16)
    gathered = lax.all_gather(divided, "aux", axis=0, tiled=True)
    return gathered[:occ_rows]


def solution(mesh):
    placed = (P("tile", None, None, None), P("aux", None, None), P("aux", None), P(), P(), P())
    return jax.shard_map(
        on_device,
        mesh=mesh,
        in_specs=placed,
        out_specs=P(None, None, "tile", None),
        check_vma=False,
    )
```

profile of v0, /device:TPU:0, one launch (start us, length us, event | category | flops | bytes accessed | tf_op | source)
XLA Modules:
  0.0 68.3 jit_solution(11172948436916942346)
XLA Ops:
  6.5 0.0 copy-start
  6.5 0.0 copy-start.4
  6.5 0.0 copy-start.1
  6.5 0.8 %compare_select_fusion = s32[8]{0:T(128)S(1)} fusion(s32[8]{0:T(128)} %param.9), kind=kLoop, calls=%fused_computation.12 | loop fusion | flops 24 | bytes 64 | tf_op jit(solution)/shard_map/jit(_take)/jit(_where)/select_n | solution.py:12
  7.3 0.0 copy-done.4
  7.3 0.2 copy-done
  7.5 0.6 gather_fusion
  8.1 0.8 %bitcast_select_fusion = bf16[1,8,128,128]{3,2,0,1:T(8,128)(2,1)} fusion(bf16[8,128,128]{2,1,0:T(8,128)(2,1)S(1)} %gather_fusion, pred[8]{0:T(512)(128)(4,1)S(1)} %compare_and_fusion), kind=kLoop, calls=%fused_computation.7 | loop fusion | flops 131072 | bytes 524296 | tf_op jit(solution)/shard_map/jit(_take)/select_n | solution.py:12
  8.9 0.0 copy-start.3
  8.9 5.3 %all-to-all-start = ((bf16[1,8,128,128]{3,2,0,1:T(8,128)(2,1)}), bf16[1,8,128,128]{3,2,0,1:T(8,128)(2,1)}, u32[]{:S(2)}, u32[]{:S(2)}) async-start(bf16[1,8,128,128]{3,2,0,1:T(8,128)(2,1)} %bitcast_select_fusion), calls=%async_computation | async-start | bytes 524288 | tf_op jit(solution)/shard_map/all_to_all | solution.py:13
  14.2 0.0 reduce-scatter.2.cloned.1.call-start
  14.3 0.0 copy-done.3
  14.3 0.0 copy-done.1
  14.3 0.7 %broadcast_multiply_fusion = bf16[512,8,128]{2,1,0:T(8,128)(2,1)S(1)} fusion(bf16[512,8,128]{2,1,0:T(8,128)(2,1)S(1)} %copy-done.1, bf16[512,8]{1,0:T(8,128)(2,1)S(1)} %bitcast.29), kind=kLoop, calls=%fused_computation.5 | loop fusion | flops 524288 | bytes 2105344 | tf_op jit(solution)/shard_map/mul | solution.py:11
  15.1 0.7 copy.9
  15.7 5.5 %all-to-all-done = bf16[1,8,128,128]{3,2,0,1:T(8,128)(2,1)} async-done(((bf16[1,8,128,128]{3,2,0,1:T(8,128)(2,1)}), bf16[1,8,128,128]{3,2,0,1:T(8,128)(2,1)}, u32[]{:S(2)}, u32[]{:S(2)}) %all-to-all-start) | async-done | bytes 262176 | tf_op jit(solution)/shard_map/all_to_all | solution.py:13
  21.2 3.1 %convolution_bitcast_fusion = f32[8,128,1,128]{3,1,0,2:T(8,128)} fusion(bf16[512,8,128]{0,2,1:T(8,128)(2,1)S(1)} %copy.9, bf16[1,8,128,128]{3,2,0,1:T(8,128)(2,1)} %all-to-all-done), kind=kOutput, calls=%fused_computation.1 | convolution fusion | flops 268500992 | bytes 1835008 | tf_op jit(solution)/shard_map/qia,qpb->iapb/dot_general | solution.py:17
  24.3 0.0 reduce-scatter.2.cloned.1.call-update
  24.3 0.6 dynamic_slice.6
  26.9 0.0 copy-start.5
  26.9 0.6 copy-done.5
  27.5 0.1 dynamic_slice.7
  27.6 0.6 dynamic-slice.2
  28.7 0.0 copy-start.2
  28.7 0.6 copy-done.2
  29.4 0.1 add_subtract_fusion
  29.4 16.5 %reduce-scatter.2.cloned.1.call-done = f32[2,128,1,128]{3,1,0,2:T(8,128)} async-done(((f32[8,128,1,128]{3,1,0,2:T(8,128)}), f32[2,128,1,128]{3,1,0,2:T(8,128)}) %reduce-scatter.2.cloned.1.call-update) | async-done | bytes 131088 | tf_op jit(solution)/shard_map/reduce_scatter | solution.py:31
  45.9 1.0 %fusion.4 = bf16[2,128,1,128]{3,1,2,0:T(8,128)(2,1)S(1)} fusion(f32[2,128,1,128]{3,1,0,2:T(8,128)} %reduce-scatter.2.cloned.1.call-done, f32[2]{0:T(128)S(1)} %dynamic_slice.7, f32[128,128]{1,0:T(8,128)S(1)} %add_subtract_fusion), kind=kLoop, calls=%fused_computation.10 | loop fusion | flops 98304 | bytes 262152 | tf_op jit(solution)/shard_map/convert_element_type | solution.py:37
  46.9 13.8 %all_gather.3 = bf16[8,128,1,128]{3,1,2,0:T(8,128)(2,1)S(1)} all-gather(bf16[2,128,1,128]{3,1,2,0:T(8,128)(2,1)S(1)} %fusion.4), channel_id=1, replica_groups=mesh['tile'=8,'aux'=4] {'aux'}, dimensions={0}, use_global_device_ids=true | all-gather | bytes 327680 | tf_op jit(solution)/shard_map/all_gather | solution.py:38
  60.7 0.7 %copy.13 = bf16[8,128,1,128]{3,1,2,0:T(8,128)(2,1)} copy(bf16[8,128,1,128]{3,1,2,0:T(8,128)(2,1)S(1)} %all_gather.3) | data formatting | bytes 524288
  (4 shorter events, 0.0 us)
Async XLA Ops:
  6.5 1.0 %copy-start = (bf16[1,8,128,128]{3,2,1,0:T(8,128)(2,1)S(1)}, bf16[1,8,128,128]{3,2,1,0:T(8,128)(2,1)}, u32[]{:S(2)}) copy-start(bf16[1,8,128,128]{3,2,1,0:T(8,128)(2,1)} %param.6) | copy-start | bytes 786436
  6.5 0.8 %copy-start.4 = (s32[8]{0:T(128)S(1)}, s32[8]{0:T(128)}, u32[]{:S(2)}) copy-start(s32[8]{0:T(128)} %param.9) | copy-start | bytes 100
  6.5 7.8 %copy-start.1 = (bf16[512,8,128]{2,1,0:T(8,128)(2,1)S(1)}, bf16[512,8,128]{2,1,0:T(8,128)(2,1)}, u32[]{:S(2)}) copy-start(bf16[512,8,128]{2,1,0:T(8,128)(2,1)} %param.7) | copy-start | bytes 3145732
  8.9 5.4 %copy-start.3 = (s32[4,8]{1,0:T(4,128)S(1)}, s32[4,8]{1,0:T(4,128)}, u32[]{:S(2)}) copy-start(s32[4,8]{1,0:T(4,128)} %param.8) | copy-start | bytes 388
  8.9 12.3 %all-to-all-start = ((bf16[1,8,128,128]{3,2,0,1:T(8,128)(2,1)}), bf16[1,8,128,128]{3,2,0,1:T(8,128)(2,1)}, u32[]{:S(2)}, u32[]{:S(2)}) async-start(bf16[1,8,128,128]{3,2,0,1:T(8,128)(2,1)} %bitcast_select_fusion), calls=%async_computation | async-start | bytes 524288 | tf_op jit(solution)/shard_map/all_to_all | solution.py:13
  14.2 31.7 %reduce-scatter.2.cloned.1.call-start = ((), (), s32[]{:S(2)}) async-start(), calls=%async_computation.2 | async-start | bytes 655360 | tf_op jit(solution)/shard_map/reduce_scatter | solution.py:31
  26.9 0.7 copy-start.5
  28.7 0.7 copy-start.2
Sparse Core Ops, SparseCore 0:
  24.4 21.4 reduce-scatter.1
where the time goes:
time: 68.6 us; the launch traced here: 68.3 us
  waiting for transfers between devices  22 us (32%)
  between operations  16 us (23%)
  blocking collectives  13.8 us (20%)
  starting transfers between devices  5.37 us (8%)
  local copies, waits for them, and re-layouts  4.7 us (7%)
  other arithmetic  3.36 us (5%)
  matrix products  3.05 us (4%)
    reduce_scatter x1, waiting for transfers between devices, on_device(): lax.psum_scatter(padded, 'aux', scatter_dimension=0, tiled=True)  16.5 us
    all_gather x1, blocking collectives, on_device(): gathered = lax.all_gather(divided, 'aux', axis=0, tiled=True)  13.8 us
    all_to_all x1, waiting for transfers between devices, on_device(): lax.all_to_all(permuted, 'tile', split_axis=1, concat_axis=0, tiled=True)  5.5 us
    all_to_all x1, starting transfers between devices, on_device(): lax.all_to_all(permuted, 'tile', split_axis=1, concat_axis=0, tiled=True)  5.33 us
    dot_general x1, matrix products, on_device(): jnp.einsum('qia,qpb->iapb', screened, intermed, preferred_element_type=jn...  3.05 us
    unnamed x13, local copies, waits for them, and re-layouts  2.19 us
    select_n x2, other arithmetic, on_device(): permuted = jnp.take(amps, owner, axis=1)  1.56 us
  transfers between devices with their start and end apart: 2, of which 2 were waited for; matrix products, arithmetic and copies ran while one was open for 4% of the time, Pallas kernels for 0%

commit v1 on v0

v1 whole, which is shorter than its diff:
```python
import functools

import jax
import jax.numpy as jnp
from jax import lax
from jax.experimental import pallas as pl
from jax.experimental.pallas import tpu as pltpu
from jax.sharding import PartitionSpec as P


def hop_to(i, k, n):
    return i ^ k if n & (n - 1) == 0 else (i + k) % n


def hop_from(i, k, n):
    return i ^ k if n & (n - 1) == 0 else (i + n - k) % n


def pack_kernel(groups, owner_ref, own_ref, mate_ref, *out_refs):
    me = lax.axis_index("tile")
    for step, out_ref in enumerate(out_refs):
        slot = 2 * hop_to(me // 2, step, groups) + me % 2
        column = owner_ref[slot]
        out_ref[0] = own_ref[column]
        out_ref[1] = mate_ref[column]


def cycle_kernel(groups, aux_count, share_rows, screened_ref, flipped_ref, *refs):
    piece_refs, out_refs, amps_ref = refs[:groups], refs[groups:-1], refs[-1]
    me = lax.axis_index("tile")
    virt = amps_ref.shape[1]
    for step, piece_ref in enumerate(piece_refs):
        group = hop_from(me // 2, step, groups)
        for part in range(2):
            k = 2 * group + (me + part) % 2
            amps_ref[pl.ds(pl.multiple_of(k * virt, virt), virt), :] = piece_ref[part]
    inter = jnp.dot(
        screened_ref[...], amps_ref[...], preferred_element_type=jnp.float32
    ).astype(jnp.bfloat16)
    block = share_rows * virt
    for step, out_ref in enumerate(out_refs):
        share = hop_to(lax.axis_index("aux"), step, aux_count)
        rows = flipped_ref[pl.ds(pl.multiple_of(share * block, block), block), :]
        partial = jnp.dot(rows, inter, preferred_element_type=jnp.float32)
        out_ref[...] = partial.reshape(out_ref.shape).astype(out_ref.dtype)


def join_kernel(aux_count, share_rows, *refs):
    piece_refs, out_ref = refs[:-1], refs[-1]
    me = lax.axis_index("aux")
    for step, piece_ref in enumerate(piece_refs):
        share = hop_from(me, step, aux_count)
        out_ref[pl.ds(share * share_rows, share_rows)] = piece_ref[...]


VMEM = pl.BlockSpec(memory_space=pltpu.VMEM)
SMEM = pl.BlockSpec(memory_space=pltpu.SMEM)


def room(bytes_used):
    return pltpu.CompilerParams(vmem_limit_bytes=bytes_used + (1 << 20))


def on_device(amps, fitted, screen, owner, eps_occ, eps_vir):
    virt = amps.shape[-1]
    aux_here, occ_rows, _ = fitted.shape
    tile_count, aux_count = lax.axis_size("tile"), lax.axis_size("aux")
    groups = tile_count // 2
    share_rows = -(-occ_rows // aux_count)
    padded_rows = share_rows * aux_count

    own = amps[0]
    mate = lax.ppermute(own, "tile", [(t, t ^ 1) for t in range(tile_count)])
    tile_piece = jax.ShapeDtypeStruct((2, virt, virt), amps.dtype)
    packed = pl.pallas_call(
        functools.partial(pack_kernel, groups),
        out_shape=[tile_piece] * groups,
        in_specs=[SMEM, VMEM, VMEM],
        out_specs=[VMEM] * groups,
        compiler_params=room(6 * own.size),
    )(owner, own, mate)
    pieces = [packed[0]] + [
        lax.ppermute(
            packed[step],
            "tile",
            [(t, 2 * hop_to(t // 2, step, groups) + t % 2) for t in range(tile_count)],
        )
        for step in range(1, groups)
    ]

    tile_mask = jnp.repeat(screen, aux_here // screen.shape[0], axis=0).astype(fitted.dtype)
    screened = fitted * tile_mask[:, :, None]
    flat = screened.reshape(aux_here, occ_rows * virt)
    flipped = jnp.pad(
        screened.transpose(1, 2, 0).reshape(occ_rows * virt, aux_here),
        ((0, (padded_rows - occ_rows) * virt), (0, 0)),
    )
    share = (share_rows, virt, virt)
    partials = pl.pallas_call(
        functools.partial(cycle_kernel, groups, aux_count, share_rows),
        out_shape=[jax.ShapeDtypeStruct(share, jnp.float32)]
        + [jax.ShapeDtypeStruct(share, jnp.bfloat16)] * (aux_count - 1),
        in_specs=[VMEM] * (2 + groups),
        out_specs=[VMEM] * aux_count,
        scratch_shapes=[pltpu.VMEM((occ_rows * virt, virt), amps.dtype)],
        compiler_params=room(2 * flat.size + 2 * flipped.size + 8 * own.size + 8 * padded_rows * virt * virt),
    )(flat, flipped, *pieces)

    def spread(value, step):
        perm = [(z, hop_to(z, step, aux_count)) for z in range(aux_count)]
        return lax.ppermute(value, "aux", perm)

    cycle = partials[0]
    for step in range(1, aux_count):
        cycle = cycle + spread(partials[step], step).astype(jnp.float32)

    own_owner = lax.dynamic_index_in_dim(owner, lax.axis_index("tile"), 0, keepdims=False)
    eps_slot = lax.dynamic_index_in_dim(eps_occ, own_owner, 0, keepdims=False)
    eps_share = lax.dynamic_slice_in_dim(
        jnp.pad(eps_occ, (0, padded_rows - occ_rows)),
        lax.axis_index("aux") * share_rows,
        share_rows,
        0,
    )
    virt_pair = eps_vir[None, :, None] + eps_vir[None, None, :] - eps_slot
    divided = (cycle / (virt_pair - eps_share[:, None, None])).astype(jnp.bfloat16)

    shares = [divided] + [spread(divided, step) for step in range(1, aux_count)]
    joined = pl.pallas_call(
        functools.partial(join_kernel, aux_count, share_rows),
        out_shape=jax.ShapeDtypeStruct((padded_rows, virt, virt), jnp.bfloat16),
        in_specs=[VMEM] * aux_count,
        compiler_params=room(8 * padded_rows * virt * virt),
    )(*shares)
    return joined[:occ_rows, :, None, :]


def solution(mesh):
    placed = (P("tile", None, None, None), P("aux", None, None), P("aux", None), P(), P(), P())
    return jax.shard_map(
        on_device,
        mesh=mesh,
        in_specs=placed,
        out_specs=P(None, None, "tile", None),
        check_vma=False,
    )
```

time: 68.6 us -> 35.7 us (0.52)
  between operations: 16 us -> 2.1 us
  blocking collectives: 13.8 us -> 0 us
  waiting for transfers between devices: 22 us -> 8.93 us
  starting transfers between devices: 5.37 us -> 13.8 us
  matrix products: 3.05 us -> 0 us
  Pallas kernels: 0 us -> 2.63 us
  local copies, waits for them, and re-layouts: 4.7 us -> 3.21 us
  other arithmetic: 3.36 us -> 4.83 us
    reduce_scatter x1 -> x0, waiting for transfers between devices: 16.5 us -> none  [on_device(): lax.psum_scatter(padded, 'aux', scatter_dimension=0, tiled=True)]
    all_gather x1 -> x0, blocking collectives: 13.8 us -> none  [on_device(): gathered = lax.all_gather(divided, 'aux', axis=0, tiled=True)]
    ppermute x0 -> x10, starting transfers between devices: none -> 13.8 us  [the longest x6 9.22 us: spread(): return lax.ppermute(value, 'aux', perm)]
    ppermute x0 -> x10, waiting for transfers between devices: none -> 8.93 us  [the longest x6 8.92 us: spread(): return lax.ppermute(value, 'aux', perm)]
    all_to_all x1 -> x0, waiting for transfers between devices: 5.5 us -> none  [on_device(): lax.all_to_all(permuted, 'tile', split_axis=1, concat_axis=0, tiled=True)]
    all_to_all x1 -> x0, starting transfers between devices: 5.33 us -> none  [on_device(): lax.all_to_all(permuted, 'tile', split_axis=1, concat_axis=0, tiled=True)]
    dot_general x1 -> x0, matrix products: 3.05 us -> none  [on_device(): jnp.einsum('qia,qpb->iapb', screened, intermed, preferred_element_type=jn...]
    pallas_call x0 -> x3, Pallas kernels: none -> 2.63 us  [the longest x1 1.32 us: on_device(): pl.pallas_call(functools.partial(cycle_kernel, groups, aux_count, share_r...]
  transfers between devices with their start and end apart: 2 -> 10, of which waited for: 2 -> 5; matrix products, arithmetic and copies ran while one was open for 4% -> 22% of each run, Pallas kernels for 0% -> 0%
where the time goes in v1:
time: 35.7 us; the launch traced here: 35.5 us
  starting transfers between devices  13.8 us (39%)
  waiting for transfers between devices  8.93 us (25%)
  other arithmetic  4.83 us (14%)
  local copies, waits for them, and re-layouts  3.21 us (9%)
  Pallas kernels  2.63 us (7%)
  between operations  2.1 us (6%)
    ppermute x6, starting transfers between devices, spread(): return lax.ppermute(value, 'aux', perm)  9.22 us
    ppermute x6, waiting for transfers between devices, spread(): return lax.ppermute(value, 'aux', perm)  8.92 us
    ppermute x3, starting transfers between devices, on_device(): lax.ppermute(packed[step], 'tile', [(t, 2 * hop_to(t // 2, step, groups)...  4.08 us
    mul x1, other arithmetic, on_device(): screened = fitted * tile_mask[:, :, None]  1.84 us
    transpose x1, local copies, waits for them, and re-layouts, on_device(): screened.transpose(1, 2, 0).reshape(occ_rows * virt, aux_here)  1.63 us
    transpose x1, other arithmetic, on_device(): screened.transpose(1, 2, 0).reshape(occ_rows * virt, aux_here)  1.48 us
    pallas_call x1, Pallas kernels, on_device(): pl.pallas_call(functools.partial(cycle_kernel, groups, aux_count, share_r...  1.32 us
    pallas_call x1, Pallas kernels, on_device(): pl.pallas_call(functools.partial(join_kernel, aux_count, share_rows), out...  0.73 us
  transfers between devices with their start and end apart: 10, of which 5 were waited for; matrix products, arithmetic and copies ran while one was open for 22% of the time, Pallas kernels for 0%

profile of v1, /device:TPU:0, one launch (start us, length us, event | category | flops | bytes accessed | tf_op | source)
XLA Modules:
  0.0 35.5 jit_solution(17349713693492862138)
XLA Ops:
  0.0 0.5 %collective-permute-start = (bf16[8,128,128]{2,1,0:T(8,128)(2,1)}, bf16[8,128,128]{2,1,0:T(8,128)(2,1)S(1)}, u32[]{:S(2)}, u32[]{:S(2)}) collective-permute-start(bf16[8,128,128]{2,1,0:T(8,128)(2,1)} %bitcast.16), channel_id=1, source_target_pairs={{0,4},{4,0},{8,12},{12,8},{16,20},{20,16},{24,28},{28,24},{1,5},{5... | collective-permute-start | bytes 786440 | tf_op jit(solution)/shard_map/ppermute | solution.py:73
  0.5 0.7 %convert_element_type.23 = bf16[4,8]{1,0:T(4,128)(2,1)S(1)} convert(s32[4,8]{1,0:T(4,128)} %param.8) | non-fusion elementwise | flops 32 | bytes 192 | tf_op jit(solution)/shard_map/convert_element_type | solution.py:91
  1.2 0.0 copy-start
  1.2 0.0 copy-start.1
  1.2 0.0 copy-start.2
  1.2 1.8 %broadcast_multiply_fusion = bf16[512,8,128]{2,1,0:T(8,128)(2,1)S(1)} fusion(bf16[512,8,128]{2,1,0:T(8,128)(2,1)} %param.7, bf16[512,8]{1,0:T(8,128)(2,1)S(1)} %bitcast.19), kind=kLoop, calls=%fused_computation.1 | loop fusion | flops 524288 | bytes 2105344 | tf_op jit(solution)/shard_map/mul | solution.py:92
  3.1 0.6 %shard_map.64 = (bf16[2,128,128]{2,1,0:T(8,128)(2,1)S(1)}, bf16[2,128,128]{2,1,0:T(8,128)(2,1)S(1)}, bf16[2,128,128]{2,1,0:T(8,128)(2,1)S(1)}, bf16[2,128,128]{2,1,0:T(8,128)(2,1)S(1)}) custom-call(s32[8]{0:T(128)S(1)} %copy-done.1, bf16[8,128,128]{2,1,0:T(8,128)(2,1)S(1)} %bitcast.17, bf16[8,128,128]{2,1,0:T(8,128)(2,1)S(1)} %collective-permute-done.mate_ref), custom_call_target="tpu_custom_call" | custom-call | tf_op jit(solution)/shard_map/pallas_call | solution.py:75
  3.7 2.5 %collective-permute-start.1 = (bf16[2,128,128]{2,1,0:T(8,128)(2,1)S(1)}, bf16[2,128,128]{2,1,0:T(8,128)(2,1)S(1)}, u32[]{:S(2)}, u32[]{:S(2)}) collective-permute-start(bf16[2,128,128]{2,1,0:T(8,128)(2,1)S(1)} %get-tuple-element.14), channel_id=1, source_target_pairs={{0,8},{4,12},{8,0},{12,4},{16,24},{20,28},{24,16},{28,20},{1,9},{5... | collective-permute-start | bytes 196616 | tf_op jit(solution)/shard_map/ppermute | solution.py:83
  6.3 1.5 %collective-permute-start.2 = (bf16[2,128,128]{2,1,0:T(8,128)(2,1)S(1)}, bf16[2,128,128]{2,1,0:T(8,128)(2,1)S(1)}, u32[]{:S(2)}, u32[]{:S(2)}) collective-permute-start(bf16[2,128,128]{2,1,0:T(8,128)(2,1)S(1)} %get-tuple-element.15), channel_id=1, source_target_pairs={{0,16},{4,20},{8,24},{12,28},{16,0},{20,4},{24,8},{28,12},{1,17},{... | collective-permute-start | bytes 196616 | tf_op jit(solution)/shard_map/ppermute | solution.py:83
  7.8 0.0 collective-permute-start.3
  7.8 1.5 %fusion = bf16[8,128,512]{1,0,2:T(8,128)(2,1)} fusion(bf16[512,8,128]{2,1,0:T(8,128)(2,1)S(1)} %copy-done.2, bf16[512,8]{1,0:T(8,128)(2,1)S(1)} %bitcast.20), kind=kLoop, calls=%fused_computation.4 | loop fusion | flops 524288 | bytes 2105344 | tf_op jit(solution)/shard_map/transpose | solution.py:95
  9.3 0.6 %dynamic_slice.11 = s32[1]{0:T(128)} dynamic-slice(s32[8]{0:T(128)S(1)} %copy-done.1, s32[]{:T(128)S(6)} %select_n.11), dynamic_slice_sizes={1} | dynamic-slice | bytes 12 | tf_op jit(solution)/shard_map/jit(dynamic_index_in_dim)/dynamic_slice | solution.py:117
  11.2 0.3 copy.11
  11.4 1.6 %copy.7 = bf16[8,128,512]{2,1,0:T(8,128)(2,1)S(1)} copy(bf16[8,128,512]{1,0,2:T(8,128)(2,1)} %fusion) | data formatting | bytes 2097152 | tf_op jit(solution)/shard_map/transpose | solution.py:95
  13.1 0.0 copy-start.4
  13.8 0.6 %dynamic_slice.12 = f32[1]{0:T(128)} dynamic-slice(f32[8]{0:T(128)S(1)} %copy-done.4, s32[]{:T(128)S(6)} %select_n.12), dynamic_slice_sizes={1} | dynamic-slice | bytes 12 | tf_op jit(solution)/shard_map/jit(dynamic_index_in_dim)/dynamic_slice | solution.py:118
  14.4 1.3 %shard_map.65 = (f32[2,128,128]{2,1,0:T(8,128)S(1)}, bf16[2,128,128]{2,1,0:T(8,128)(2,1)S(1)}, bf16[2,128,128]{2,1,0:T(8,128)(2,1)S(1)}, bf16[2,128,128]{2,1,0:T(8,128)(2,1)S(1)}) custom-call(bf16[512,1024]{1,0:T(8,128)(2,1)S(1)} %bitcast.14, bf16[1024,512]{1,0:T(8,128)(2,1)S(1)} %bitcast.15, bf16[2,128,128]{2,1,0:T(8,128)(2,1)S(1)} %get-tuple-element.13.refs_0_, ...), custom_call_target="tpu_custom_call" | custom-call | tf_op jit(solution)/shard_map/pallas_call | solution.py:99
  15.7 4.1 %collective-permute-start.6 = (bf16[2,128,128]{2,1,0:T(8,128)(2,1)S(1)}, bf16[2,128,128]{2,1,0:T(8,128)(2,1)S(1)}, u32[]{:S(2)}, u32[]{:S(2)}) collective-permute-start(bf16[2,128,128]{2,1,0:T(8,128)(2,1)S(1)} %get-tuple-element.20), channel_id=1, source_target_pairs={{0,3},{1,2},{2,1},{3,0},{4,7},{5,6},{6,5},{7,4},{8,11},{9,10},{10,... | collective-permute-start | bytes 196616 | tf_op jit(solution)/shard_map/ppermute | solution.py:111
  19.8 0.6 %collective-permute-start.4 = (bf16[2,128,128]{2,1,0:T(8,128)(2,1)S(1)}, bf16[2,128,128]{2,1,0:T(8,128)(2,1)S(1)}, u32[]{:S(2)}, u32[]{:S(2)}) collective-permute-start(bf16[2,128,128]{2,1,0:T(8,128)(2,1)S(1)} %get-tuple-element.18), channel_id=1, source_target_pairs={{0,1},{1,0},{2,3},{3,2},{4,5},{5,4},{6,7},{7,6},{8,9},{9,8},{10,11... | collective-permute-start | bytes 196616 | tf_op jit(solution)/shard_map/ppermute | solution.py:111
  20.5 0.0 copy-done.3
  20.5 0.7 %add_subtract_fusion = f32[128,128]{1,0:T(8,128)S(1)} fusion(f32[]{:T(128)} %bitcast.5, f32[128]{0:T(128)S(1)} %copy-done.3), kind=kLoop, calls=%fused_computation.3 | loop fusion | flops 32768 | bytes 66052 | tf_op jit(solution)/shard_map/sub | solution.py:125
  21.2 0.1 dynamic_slice.13
  21.3 1.2 %collective-permute-done.6 = bf16[2,128,128]{2,1,0:T(8,128)(2,1)S(1)} collective-permute-done((bf16[2,128,128]{2,1,0:T(8,128)(2,1)S(1)}, bf16[2,128,128]{2,1,0:T(8,128)(2,1)S(1)}, u32[]{:S(2)}, u32[]{:S(2)}) %collective-permute-start.6) | collective-permute-done | bytes 65568 | tf_op jit(solution)/shard_map/ppermute | solution.py:111
  22.4 2.8 %collective-permute-done.5 = bf16[2,128,128]{2,1,0:T(8,128)(2,1)S(1)} collective-permute-done((bf16[2,128,128]{2,1,0:T(8,128)(2,1)S(1)}, bf16[2,128,128]{2,1,0:T(8,128)(2,1)S(1)}, u32[]{:S(2)}, u32[]{:S(2)}) %collective-permute-start.5) | collective-permute-done | bytes 65568 | tf_op jit(solution)/shard_map/ppermute | solution.py:111
  25.2 0.1 divide_convert_fusion.refs_0_
  25.3 1.1 %collective-permute-start.7 = (bf16[2,128,128]{2,1,0:T(8,128)(2,1)S(1)}, bf16[2,128,128]{2,1,0:T(8,128)(2,1)S(1)}, u32[]{:S(2)}, u32[]{:S(2)}) collective-permute-start(bf16[2,128,128]{2,1,0:T(8,128)(2,1)S(1)} %divide_convert_fusion.refs_0_), channel_id=1, source_target_pairs={{0,1},{1,0},{2,3},{3,2},{4,5},{5,4},{6,7},{7,6},{8,9},{9,8},{10,11... | collective-permute-start | bytes 196616 | tf_op jit(solution)/shard_map/ppermute | solution.py:111
  26.5 2.2 %collective-permute-start.8 = (bf16[2,128,128]{2,1,0:T(8,128)(2,1)S(1)}, bf16[2,128,128]{2,1,0:T(8,128)(2,1)S(1)}, u32[]{:S(2)}, u32[]{:S(2)}) collective-permute-start(bf16[2,128,128]{2,1,0:T(8,128)(2,1)S(1)} %divide_convert_fusion.refs_0_), channel_id=1, source_target_pairs={{0,2},{1,3},{2,0},{3,1},{4,6},{5,7},{6,4},{7,5},{8,10},{9,11},{10,... | collective-permute-start | bytes 196616 | tf_op jit(solution)/shard_map/ppermute | solution.py:111
  28.7 1.1 %collective-permute-start.9 = (bf16[2,128,128]{2,1,0:T(8,128)(2,1)S(1)}, bf16[2,128,128]{2,1,0:T(8,128)(2,1)S(1)}, u32[]{:S(2)}, u32[]{:S(2)}) collective-permute-start(bf16[2,128,128]{2,1,0:T(8,128)(2,1)S(1)} %divide_convert_fusion.refs_0_), channel_id=1, source_target_pairs={{0,3},{1,2},{2,1},{3,0},{4,7},{5,6},{6,5},{7,4},{8,11},{9,10},{10,... | collective-permute-start | bytes 196616 | tf_op jit(solution)/shard_map/ppermute | solution.py:111
  29.8 0.3 collective-permute-done.7.refs_1_
  30.1 2.9 %collective-permute-done.8.refs_2_ = bf16[2,128,128]{2,1,0:T(8,128)(2,1)S(1)} collective-permute-done((bf16[2,128,128]{2,1,0:T(8,128)(2,1)S(1)}, bf16[2,128,128]{2,1,0:T(8,128)(2,1)S(1)}, u32[]{:S(2)}, u32[]{:S(2)}) %collective-permute-start.8) | collective-permute-done | bytes 65568 | tf_op jit(solution)/shard_map/ppermute | solution.py:111
  33.0 1.8 %collective-permute-done.9.refs_3_ = bf16[2,128,128]{2,1,0:T(8,128)(2,1)S(1)} collective-permute-done((bf16[2,128,128]{2,1,0:T(8,128)(2,1)S(1)}, bf16[2,128,128]{2,1,0:T(8,128)(2,1)S(1)}, u32[]{:S(2)}, u32[]{:S(2)}) %collective-permute-start.9) | collective-permute-done | bytes 65568 | tf_op jit(solution)/shard_map/ppermute | solution.py:111
  34.8 0.7 %shard_map.66 = bf16[8,128,128]{2,1,0:T(8,128)(2,1)} custom-call(bf16[2,128,128]{2,1,0:T(8,128)(2,1)S(1)} %divide_convert_fusion.refs_0_, bf16[2,128,128]{2,1,0:T(8,128)(2,1)S(1)} %collective-permute-done.7.refs_1_, bf16[2,128,128]{2,1,0:T(8,128)(2,1)S(1)} %collective-permute-done.8.refs_2_, bf16[2,128,128]{2,1,0:T(8,128)(2,1)S(1)} %collective-permute-done.9.refs_3_), custom_call_target="tpu_custom_call" | custom-call | tf_op jit(solution)/shard_map/pallas_call | solution.py:129
  (12 shorter events, 0.0 us)
Async XLA Ops:
  0.0 3.1 %collective-permute-start = (bf16[8,128,128]{2,1,0:T(8,128)(2,1)}, bf16[8,128,128]{2,1,0:T(8,128)(2,1)S(1)}, u32[]{:S(2)}, u32[]{:S(2)}) collective-permute-start(bf16[8,128,128]{2,1,0:T(8,128)(2,1)} %bitcast.16), channel_id=1, source_target_pairs={{0,4},{4,0},{8,12},{12,8},{16,20},{20,16},{24,28},{28,24},{1,5},{5... | collective-permute-start | bytes 786440 | tf_op jit(solution)/shard_map/ppermute | solution.py:73
  1.2 1.9 %copy-start = (bf16[1,8,128,128]{3,2,1,0:T(8,128)(2,1)S(1)}, bf16[1,8,128,128]{3,2,1,0:T(8,128)(2,1)}, u32[]{:S(2)}) copy-start(bf16[1,8,128,128]{3,2,1,0:T(8,128)(2,1)} %param.6) | copy-start | bytes 786436
  1.2 1.9 %copy-start.1 = (s32[8]{0:T(128)S(1)}, s32[8]{0:T(128)}, u32[]{:S(2)}) copy-start(s32[8]{0:T(128)} %owner_ref.1) | copy-start | bytes 100
  1.2 6.6 %copy-start.2 = (bf16[512,8,128]{2,1,0:T(8,128)(2,1)S(1)}, bf16[512,8,128]{2,1,0:T(8,128)(2,1)}, u32[]{:S(2)}) copy-start(bf16[512,8,128]{2,1,0:T(8,128)(2,1)} %param.7) | copy-start | bytes 3145732
  3.7 10.6 %collective-permute-start.1 = (bf16[2,128,128]{2,1,0:T(8,128)(2,1)S(1)}, bf16[2,128,128]{2,1,0:T(8,128)(2,1)S(1)}, u32[]{:S(2)}, u32[]{:S(2)}) collective-permute-start(bf16[2,128,128]{2,1,0:T(8,128)(2,1)S(1)} %get-tuple-element.14), channel_id=1, source_target_pairs={{0,8},{4,12},{8,0},{12,4},{16,24},{20,28},{24,16},{28,20},{1,9},{5... | collective-permute-start | bytes 196616 | tf_op jit(solution)/shard_map/ppermute | solution.py:83
  6.3 8.1 %collective-permute-start.2 = (bf16[2,128,128]{2,1,0:T(8,128)(2,1)S(1)}, bf16[2,128,128]{2,1,0:T(8,128)(2,1)S(1)}, u32[]{:S(2)}, u32[]{:S(2)}) collective-permute-start(bf16[2,128,128]{2,1,0:T(8,128)(2,1)S(1)} %get-tuple-element.15), channel_id=1, source_target_pairs={{0,16},{4,20},{8,24},{12,28},{16,0},{20,4},{24,8},{28,12},{1,17},{... | collective-permute-start | bytes 196616 | tf_op jit(solution)/shard_map/ppermute | solution.py:83
  7.8 6.6 %collective-permute-start.3 = (bf16[2,128,128]{2,1,0:T(8,128)(2,1)S(1)}, bf16[2,128,128]{2,1,0:T(8,128)(2,1)S(1)}, u32[]{:S(2)}, u32[]{:S(2)}) collective-permute-start(bf16[2,128,128]{2,1,0:T(8,128)(2,1)S(1)} %get-tuple-element.16), channel_id=1, source_target_pairs={{0,24},{4,28},{8,16},{12,20},{16,8},{20,12},{24,0},{28,4},{1,25},{... | collective-permute-start | bytes 196616 | tf_op jit(solution)/shard_map/ppermute | solution.py:83
  13.1 0.7 %copy-start.4 = (f32[8]{0:T(128)S(1)}, f32[8]{0:T(128)}, u32[]{:S(2)}) copy-start(f32[8]{0:T(128)} %param.10) | copy-start | bytes 100
  15.7 6.7 %collective-permute-start.6 = (bf16[2,128,128]{2,1,0:T(8,128)(2,1)S(1)}, bf16[2,128,128]{2,1,0:T(8,128)(2,1)S(1)}, u32[]{:S(2)}, u32[]{:S(2)}) collective-permute-start(bf16[2,128,128]{2,1,0:T(8,128)(2,1)S(1)} %get-tuple-element.20), channel_id=1, source_target_pairs={{0,3},{1,2},{2,1},{3,0},{4,7},{5,6},{6,5},{7,4},{8,11},{9,10},{10,... | collective-permute-start | bytes 196616 | tf_op jit(solution)/shard_map/ppermute | solution.py:111
  19.8 5.4 %collective-permute-start.5 = (bf16[2,128,128]{2,1,0:T(8,128)(2,1)S(1)}, bf16[2,128,128]{2,1,0:T(8,128)(2,1)S(1)}, u32[]{:S(2)}, u32[]{:S(2)}) collective-permute-start(bf16[2,128,128]{2,1,0:T(8,128)(2,1)S(1)} %get-tuple-element.19), channel_id=1, source_target_pairs={{0,2},{1,3},{2,0},{3,1},{4,6},{5,7},{6,4},{7,5},{8,10},{9,11},{10,... | collective-permute-start | bytes 196616 | tf_op jit(solution)/shard_map/ppermute | solution.py:111
  19.8 0.7 %copy-start.3 = (f32[128]{0:T(128)S(1)}, f32[128]{0:T(128)}, u32[]{:S(2)}) copy-start(f32[128]{0:T(128)} %param.11) | copy-start | bytes 1540
  19.8 5.4 %collective-permute-start.4 = (bf16[2,128,128]{2,1,0:T(8,128)(2,1)S(1)}, bf16[2,128,128]{2,1,0:T(8,128)(2,1)S(1)}, u32[]{:S(2)}, u32[]{:S(2)}) collective-permute-start(bf16[2,128,128]{2,1,0:T(8,128)(2,1)S(1)} %get-tuple-element.18), channel_id=1, source_target_pairs={{0,1},{1,0},{2,3},{3,2},{4,5},{5,4},{6,7},{7,6},{8,9},{9,8},{10,11... | collective-permute-start | bytes 196616 | tf_op jit(solution)/shard_map/ppermute | solution.py:111
  25.3 4.7 %collective-permute-start.7 = (bf16[2,128,128]{2,1,0:T(8,128)(2,1)S(1)}, bf16[2,128,128]{2,1,0:T(8,128)(2,1)S(1)}, u32[]{:S(2)}, u32[]{:S(2)}) collective-permute-start(bf16[2,128,128]{2,1,0:T(8,128)(2,1)S(1)} %divide_convert_fusion.refs_0_), channel_id=1, source_target_pairs={{0,1},{1,0},{2,3},{3,2},{4,5},{5,4},{6,7},{7,6},{8,9},{9,8},{10,11... | collective-permute-start | bytes 196616 | tf_op jit(solution)/shard_map/ppermute | solution.py:111
  26.5 6.5 %collective-permute-start.8 = (bf16[2,128,128]{2,1,0:T(8,128)(2,1)S(1)}, bf16[2,128,128]{2,1,0:T(8,128)(2,1)S(1)}, u32[]{:S(2)}, u32[]{:S(2)}) collective-permute-start(bf16[2,128,128]{2,1,0:T(8,128)(2,1)S(1)} %divide_convert_fusion.refs_0_), channel_id=1, source_target_pairs={{0,2},{1,3},{2,0},{3,1},{4,6},{5,7},{6,4},{7,5},{8,10},{9,11},{10,... | collective-permute-start | bytes 196616 | tf_op jit(solution)/shard_map/ppermute | solution.py:111
  28.7 6.1 %collective-permute-start.9 = (bf16[2,128,128]{2,1,0:T(8,128)(2,1)S(1)}, bf16[2,128,128]{2,1,0:T(8,128)(2,1)S(1)}, u32[]{:S(2)}, u32[]{:S(2)}) collective-permute-start(bf16[2,128,128]{2,1,0:T(8,128)(2,1)S(1)} %divide_convert_fusion.refs_0_), channel_id=1, source_target_pairs={{0,3},{1,2},{2,1},{3,0},{4,7},{5,6},{6,5},{7,4},{8,11},{9,10},{10,... | collective-permute-start | bytes 196616 | tf_op jit(solution)/shard_map/ppermute | solution.py:111

commit v2 on v1

--- a/solution.py
+++ b/solution.py
@@ -25,10 +25,27 @@
         out_ref[1] = mate_ref[column]
 
 
-def cycle_kernel(groups, aux_count, share_rows, screened_ref, flipped_ref, *refs):
+def screen_kernel(flat_ref, screen_ref, owner_ref, eps_occ_ref, eps_vir_ref, out_ref, denominator_ref):
+    blocks, occ_rows = screen_ref.shape
+    share_rows, virt, _ = denominator_ref.shape
+    size = flat_ref.shape[0] // blocks
+    for block in range(blocks):
+        for k in range(occ_rows):
+            where = (pl.ds(block * size, size), pl.ds(k * virt, virt))
+            tile = flat_ref[where]
+            out_ref[where] = jnp.where(screen_ref[block, k] != 0, tile, jnp.zeros_like(tile))
+    eps_row = jnp.broadcast_to(eps_vir_ref[...], (virt, virt))
+    eps_slot = eps_occ_ref[owner_ref[lax.axis_index("tile")]]
+    virt_pair = eps_row.T + eps_row - eps_slot
+    for row in range(share_rows):
+        i = jnp.minimum(lax.axis_index("aux") * share_rows + row, occ_rows - 1)
+        denominator_ref[row] = virt_pair - eps_occ_ref[i]
+
+
+def cycle_kernel(groups, aux_count, screened_ref, *refs):
     piece_refs, out_refs, amps_ref = refs[:groups], refs[groups:-1], refs[-1]
     me = lax.axis_index("tile")
-    virt = amps_ref.shape[1]
+    occ_rows, virt = screened_ref.shape[1] // amps_ref.shape[1], amps_ref.shape[1]
     for step, piece_ref in enumerate(piece_refs):
         group = hop_from(me // 2, step, groups)
         for part in range(2):
@@ -37,12 +54,17 @@
     inter = jnp.dot(
         screened_ref[...], amps_ref[...], preferred_element_type=jnp.float32
     ).astype(jnp.bfloat16)
-    block = share_rows * virt
+    share_rows = out_refs[0].shape[0]
+    last = (occ_rows - share_rows) * virt
     for step, out_ref in enumerate(out_refs):
         share = hop_to(lax.axis_index("aux"), step, aux_count)
-        rows = flipped_ref[pl.ds(pl.multiple_of(share * block, block), block), :]
-        partial = jnp.dot(rows, inter, preferred_element_type=jnp.float32)
-        out_ref[...] = partial.reshape(out_ref.shape).astype(out_ref.dtype)
+        start = jnp.minimum(share * share_rows * virt, last)
+        columns = screened_ref[:, pl.ds(pl.multiple_of(start, virt), share_rows * virt)]
+        flipped = lax.dot_general(
+            inter, columns, (((0,), (0,)), ((), ())), preferred_element_type=jnp.float32
+        )
+        for row in range(share_rows):
+            out_ref[row] = flipped[:, row * virt : (row + 1) * virt].T.astype(out_ref.dtype)
 
 
 def join_kernel(aux_count, share_rows, *refs):
@@ -71,9 +93,12 @@
 
     own = amps[0]
     mate = lax.ppermute(own, "tile", [(t, t ^ 1) for t in range(tile_count)])
+    flat = fitted.reshape(aux_here, occ_rows * virt)
+    mate, flat = lax.optimization_barrier((mate, flat))
     tile_piece = jax.ShapeDtypeStruct((2, virt, virt), amps.dtype)
     packed = pl.pallas_call(
         functools.partial(pack_kernel, groups),
+        name="pack",
         out_shape=[tile_piece] * groups,
         in_specs=[SMEM, VMEM, VMEM],
         out_specs=[VMEM] * groups,
@@ -88,23 +113,28 @@
         for step in range(1, groups)
     ]
 
-    tile_mask = jnp.repeat(screen, aux_here // screen.shape[0], axis=0).astype(fitted.dtype)
-    screened = fitted * tile_mask[:, :, None]
-    flat = screened.reshape(aux_here, occ_rows * virt)
-    flipped = jnp.pad(
-        screened.transpose(1, 2, 0).reshape(occ_rows * virt, aux_here),
-        ((0, (padded_rows - occ_rows) * virt), (0, 0)),
-    )
     share = (share_rows, virt, virt)
+    screened, denominator = pl.pallas_call(
+        screen_kernel,
+        name="screen",
+        out_shape=[
+            jax.ShapeDtypeStruct(flat.shape, flat.dtype),
+            jax.ShapeDtypeStruct(share, jnp.float32),
+        ],
+        in_specs=[VMEM, SMEM, SMEM, SMEM, VMEM],
+        out_specs=[VMEM, VMEM],
+        compiler_params=room(4 * flat.size + 4 * share_rows * virt * virt),
+    )(flat, screen, owner, eps_occ, eps_vir[None, :])
     partials = pl.pallas_call(
-        functools.partial(cycle_kernel, groups, aux_count, share_rows),
+        functools.partial(cycle_kernel, groups, aux_count),
+        name="cycle",
         out_shape=[jax.ShapeDtypeStruct(share, jnp.float32)]
         + [jax.ShapeDtypeStruct(share, jnp.bfloat16)] * (aux_count - 1),
-        in_specs=[VMEM] * (2 + groups),
+        in_specs=[VMEM] * (1 + groups),
         out_specs=[VMEM] * aux_count,
         scratch_shapes=[pltpu.VMEM((occ_rows * virt, virt), amps.dtype)],
-        compiler_params=room(2 * flat.size + 2 * flipped.size + 8 * own.size + 8 * padded_rows * virt * virt),
-    )(flat, flipped, *pieces)
+        compiler_params=room(4 * flat.size + 8 * own.size + 8 * padded_rows * virt * virt),
+    )(screened, *pieces)
 
     def spread(value, step):
         perm = [(z, hop_to(z, step, aux_count)) for z in range(aux_count)]
@@ -114,20 +144,12 @@
     for step in range(1, aux_count):
         cycle = cycle + spread(partials[step], step).astype(jnp.float32)
 
-    own_owner = lax.dynamic_index_in_dim(owner, lax.axis_index("tile"), 0, keepdims=False)
-    eps_slot = lax.dynamic_index_in_dim(eps_occ, own_owner, 0, keepdims=False)
-    eps_share = lax.dynamic_slice_in_dim(
-        jnp.pad(eps_occ, (0, padded_rows - occ_rows)),
-        lax.axis_index("aux") * share_rows,
-        share_rows,
-        0,
-    )
-    virt_pair = eps_vir[None, :, None] + eps_vir[None, None, :] - eps_slot
-    divided = (cycle / (virt_pair - eps_share[:, None, None])).astype(jnp.bfloat16)
+    divided = (cycle / denominator).astype(jnp.bfloat16)
 
     shares = [divided] + [spread(divided, step) for step in range(1, aux_count)]
     joined = pl.pallas_call(
         functools.partial(join_kernel, aux_count, share_rows),
+        name="join",
         out_shape=jax.ShapeDtypeStruct((padded_rows, virt, virt), jnp.bfloat16),
         in_specs=[VMEM] * aux_count,
         compiler_params=room(8 * padded_rows * virt * virt),

time: 35.7 us -> 32.4 us (0.908)
  other arithmetic: 4.83 us -> 0.05 us
  waiting for transfers between devices: 8.93 us -> 12.5 us
  between operations: 2.1 us -> 0.08 us
  Pallas kernels: 2.63 us -> 3.32 us
  local copies, waits for them, and re-layouts: 3.21 us -> 2.79 us
    ppermute x3, waiting for transfers between devices: 0.01 us -> 3.52 us  [on_device(): lax.ppermute(packed[step], 'tile', [(t, 2 * hop_to(t // 2, step, groups)...]
    unnamed x11, local copies, waits for them, and re-layouts: 0.31 us -> 2.79 us
    mul x1 -> x0, other arithmetic: 1.84 us -> none  [on_device(): screened = fitted * tile_mask[:, :, None]]
    transpose x1 -> x0, local copies, waits for them, and re-layouts: 1.63 us -> none  [on_device(): screened.transpose(1, 2, 0).reshape(occ_rows * virt, aux_here)]
    transpose x1 -> x0, other arithmetic: 1.48 us -> none  [on_device(): screened.transpose(1, 2, 0).reshape(occ_rows * virt, aux_here)]
    dynamic_slice x3 -> x0, local copies, waits for them, and re-layouts: 1.24 us -> none  [the longest x1 0.59 us: on_device(): eps_slot = lax.dynamic_index_in_dim(eps_occ, own_owner, 0, keepdims=False)]
    convert_element_type x2 -> x1, other arithmetic: 0.78 us -> 0.05 us  [on_device(): divided = (cycle / denominator).astype(jnp.bfloat16)]
    sub x1 -> x0, other arithmetic: 0.72 us -> none  [on_device(): virt_pair = eps_vir[None, :, None] + eps_vir[None, None, :] - eps_slot]
  transfers between devices with their start and end apart: 10 -> 10, of which waited for: 5 -> 7; matrix products, arithmetic and copies ran while one was open for 22% -> 5% of each run, Pallas kernels for 0% -> 3%
where the time goes in v2:
time: 32.4 us; the launch traced here: 32.2 us
  starting transfers between devices  13.5 us (42%)
  waiting for transfers between devices  12.5 us (39%)
  Pallas kernels  3.32 us (10%)
  local copies, waits for them, and re-layouts  2.79 us (9%)
    ppermute x6, waiting for transfers between devices, spread(): return lax.ppermute(value, 'aux', perm)  8.94 us
    ppermute x6, starting transfers between devices, spread(): return lax.ppermute(value, 'aux', perm)  8.9 us
    ppermute x3, starting transfers between devices, on_device(): lax.ppermute(packed[step], 'tile', [(t, 2 * hop_to(t // 2, step, groups)...  4.11 us
    ppermute x3, waiting for transfers between devices, on_device(): lax.ppermute(packed[step], 'tile', [(t, 2 * hop_to(t // 2, step, groups)...  3.52 us
    unnamed x11, local copies, waits for them, and re-layouts  2.79 us
    pallas_call x1, Pallas kernels, on_device(): pl.pallas_call(functools.partial(cycle_kernel, groups, aux_count), name='...  1.05 us
    pallas_call x1, Pallas kernels, on_device(): pl.pallas_call(screen_kernel, name='screen', out_shape=[jax.ShapeDtypeStr...  0.96 us
    pallas_call x1, Pallas kernels, on_device(): pl.pallas_call(functools.partial(join_kernel, aux_count, share_rows), nam...  0.73 us
  transfers between devices with their start and end apart: 10, of which 7 were waited for; matrix products, arithmetic and copies ran while one was open for 5% of the time, Pallas kernels for 3%

profile of v2, /device:TPU:0, one launch (start us, length us, event | category | flops | bytes accessed | tf_op | source)
XLA Modules:
  0.0 32.2 jit_solution(17801645734141009301)
XLA Ops:
  0.0 0.5 %collective-permute-start = (bf16[8,128,128]{2,1,0:T(8,128)(2,1)}, bf16[8,128,128]{2,1,0:T(8,128)(2,1)S(1)}, u32[]{:S(2)}, u32[]{:S(2)}) collective-permute-start(bf16[8,128,128]{2,1,0:T(8,128)(2,1)} %bitcast.10), channel_id=1, source_target_pairs={{0,4},{4,0},{8,12},{12,8},{16,20},{20,16},{24,28},{28,24},{1,5},{5... | collective-permute-start | bytes 786440 | tf_op jit(solution)/shard_map/ppermute | solution.py:95
  0.5 0.0 copy-start
  0.5 1.5 %copy.10 = bf16[64,8,8,128]{3,1,2,0:T(8,128)(2,1)S(1)} copy(bf16[64,8,8,128]{3,2,1,0:T(8,128)(2,1)} %bitcast.13) | data formatting | bytes 2097152
  2.0 0.0 copy-start.2
  2.0 0.0 collective-permute-done.mate_ref
  2.1 0.0 copy-done
  2.1 0.6 %copy-done.2 = s32[8]{0:T(128)S(1)} copy-done((s32[8]{0:T(128)S(1)}, s32[8]{0:T(128)}, u32[]{:S(2)}) %copy-start.2) | copy-done | bytes 56
  2.7 0.6 %pack.1 = (bf16[2,128,128]{2,1,0:T(8,128)(2,1)S(1)}, bf16[2,128,128]{2,1,0:T(8,128)(2,1)S(1)}, bf16[2,128,128]{2,1,0:T(8,128)(2,1)S(1)}, bf16[2,128,128]{2,1,0:T(8,128)(2,1)S(1)}) custom-call(s32[8]{0:T(128)S(1)} %copy-done.2, bf16[8,128,128]{2,1,0:T(8,128)(2,1)S(1)} %bitcast.11, bf16[8,128,128]{2,1,0:T(8,128)(2,1)S(1)} %collective-permute-done.mate_ref), custom_call_target="tpu_custom_call" | custom-call | tf_op jit(solution)/shard_map/pack/pallas_call | solution.py:99
  3.3 2.5 %collective-permute-start.1 = (bf16[2,128,128]{2,1,0:T(8,128)(2,1)S(1)}, bf16[2,128,128]{2,1,0:T(8,128)(2,1)S(1)}, u32[]{:S(2)}, u32[]{:S(2)}) collective-permute-start(bf16[2,128,128]{2,1,0:T(8,128)(2,1)S(1)} %get-tuple-element.21), channel_id=1, source_target_pairs={{0,8},{4,12},{8,0},{12,4},{16,24},{20,28},{24,16},{28,20},{1,9},{5... | collective-permute-start | bytes 196616 | tf_op jit(solution)/shard_map/ppermute | solution.py:108
  5.8 1.5 %collective-permute-start.2 = (bf16[2,128,128]{2,1,0:T(8,128)(2,1)S(1)}, bf16[2,128,128]{2,1,0:T(8,128)(2,1)S(1)}, u32[]{:S(2)}, u32[]{:S(2)}) collective-permute-start(bf16[2,128,128]{2,1,0:T(8,128)(2,1)S(1)} %get-tuple-element.22), channel_id=1, source_target_pairs={{0,16},{4,20},{8,24},{12,28},{16,0},{20,4},{24,8},{28,12},{1,17},{... | collective-permute-start | bytes 196616 | tf_op jit(solution)/shard_map/ppermute | solution.py:108
  7.4 0.0 collective-permute-start.3
  7.4 0.0 copy-done.1
  7.4 0.6 %copy-done.3 = f32[8]{0:T(128)S(1)} copy-done((f32[8]{0:T(128)S(1)}, f32[8]{0:T(128)}, u32[]{:S(2)}) %copy-start.3) | copy-done | bytes 56
  8.0 0.0 copy-done.4
  8.0 1.0 %screen.1 = (bf16[512,1024]{1,0:T(8,128)(2,1)S(1)}, f32[2,128,128]{2,1,0:T(8,128)S(1)}) custom-call(bf16[512,1024]{1,0:T(8,128)(2,1)S(1)} %bitcast.9, s32[4,8]{1,0:T(4,128)S(1)} %copy-done.1, s32[8]{0:T(128)S(1)} %copy-done.2, f32[8]{0:T(128)S(1)} %copy-done.3, f32[1,128]{1,0:T(1,128)S(1)} %bitcast.12), custom_call_target="tpu_custom_call" | custom-call | tf_op jit(solution)/shard_map/screen/pallas_call | solution.py:117
  9.0 0.0 collective-permute-done.1.refs_1_
  9.0 1.1 %collective-permute-done.2.refs_2_ = bf16[2,128,128]{2,1,0:T(8,128)(2,1)S(1)} collective-permute-done((bf16[2,128,128]{2,1,0:T(8,128)(2,1)S(1)}, bf16[2,128,128]{2,1,0:T(8,128)(2,1)S(1)}, u32[]{:S(2)}, u32[]{:S(2)}) %collective-permute-start.2) | collective-permute-done | bytes 65568 | tf_op jit(solution)/shard_map/ppermute | solution.py:108
  10.1 2.4 %collective-permute-done.3.refs_3_ = bf16[2,128,128]{2,1,0:T(8,128)(2,1)S(1)} collective-permute-done((bf16[2,128,128]{2,1,0:T(8,128)(2,1)S(1)}, bf16[2,128,128]{2,1,0:T(8,128)(2,1)S(1)}, u32[]{:S(2)}, u32[]{:S(2)}) %collective-permute-start.3) | collective-permute-done | bytes 65568 | tf_op jit(solution)/shard_map/ppermute | solution.py:108
  12.5 1.1 %cycle.1 = (f32[2,128,128]{2,1,0:T(8,128)S(1)}, bf16[2,128,128]{2,1,0:T(8,128)(2,1)S(1)}, bf16[2,128,128]{2,1,0:T(8,128)(2,1)S(1)}, bf16[2,128,128]{2,1,0:T(8,128)(2,1)S(1)}) custom-call(bf16[512,1024]{1,0:T(8,128)(2,1)S(1)} %get-tuple-element.18.screened_ref, bf16[2,128,128]{2,1,0:T(8,128)(2,1)S(1)} %get-tuple-element.20.refs_0_, ...), custom_call_target="tpu_custom_call" | custom-call | tf_op jit(solution)/shard_map/cycle/pallas_call | solution.py:128
  13.6 1.6 %collective-permute-start.4 = (bf16[2,128,128]{2,1,0:T(8,128)(2,1)S(1)}, bf16[2,128,128]{2,1,0:T(8,128)(2,1)S(1)}, u32[]{:S(2)}, u32[]{:S(2)}) collective-permute-start(bf16[2,128,128]{2,1,0:T(8,128)(2,1)S(1)} %get-tuple-element.25), channel_id=1, source_target_pairs={{0,1},{1,0},{2,3},{3,2},{4,5},{5,4},{6,7},{7,6},{8,9},{9,8},{10,11... | collective-permute-start | bytes 196616 | tf_op jit(solution)/shard_map/ppermute | solution.py:141
  15.2 2.6 %collective-permute-start.5 = (bf16[2,128,128]{2,1,0:T(8,128)(2,1)S(1)}, bf16[2,128,128]{2,1,0:T(8,128)(2,1)S(1)}, u32[]{:S(2)}, u32[]{:S(2)}) collective-permute-start(bf16[2,128,128]{2,1,0:T(8,128)(2,1)S(1)} %get-tuple-element.26), channel_id=1, source_target_pairs={{0,2},{1,3},{2,0},{3,1},{4,6},{5,7},{6,4},{7,5},{8,10},{9,11},{10,... | collective-permute-start | bytes 196616 | tf_op jit(solution)/shard_map/ppermute | solution.py:141
  17.8 0.2 collective-permute-start.6
  18.0 0.5 %collective-permute-done.4 = bf16[2,128,128]{2,1,0:T(8,128)(2,1)S(1)} collective-permute-done((bf16[2,128,128]{2,1,0:T(8,128)(2,1)S(1)}, bf16[2,128,128]{2,1,0:T(8,128)(2,1)S(1)}, u32[]{:S(2)}, u32[]{:S(2)}) %collective-permute-start.4) | collective-permute-done | bytes 65568 | tf_op jit(solution)/shard_map/ppermute | solution.py:141
  18.5 3.2 %collective-permute-done.5 = bf16[2,128,128]{2,1,0:T(8,128)(2,1)S(1)} collective-permute-done((bf16[2,128,128]{2,1,0:T(8,128)(2,1)S(1)}, bf16[2,128,128]{2,1,0:T(8,128)(2,1)S(1)}, u32[]{:S(2)}, u32[]{:S(2)}) %collective-permute-start.5) | collective-permute-done | bytes 65568 | tf_op jit(solution)/shard_map/ppermute | solution.py:141
  21.8 2.1 %collective-permute-done.6 = bf16[2,128,128]{2,1,0:T(8,128)(2,1)S(1)} collective-permute-done((bf16[2,128,128]{2,1,0:T(8,128)(2,1)S(1)}, bf16[2,128,128]{2,1,0:T(8,128)(2,1)S(1)}, u32[]{:S(2)}, u32[]{:S(2)}) %collective-permute-start.6) | collective-permute-done | bytes 65568 | tf_op jit(solution)/shard_map/ppermute | solution.py:141
  23.9 1.2 %collective-permute-start.9 = (bf16[2,128,128]{2,1,0:T(8,128)(2,1)S(1)}, bf16[2,128,128]{2,1,0:T(8,128)(2,1)S(1)}, u32[]{:S(2)}, u32[]{:S(2)}) collective-permute-start(bf16[2,128,128]{2,1,0:T(8,128)(2,1)S(1)} %divide_convert_fusion.refs_0_), channel_id=1, source_target_pairs={{0,3},{1,2},{2,1},{3,0},{4,7},{5,6},{6,5},{7,4},{8,11},{9,10},{10,... | collective-permute-start | bytes 196616 | tf_op jit(solution)/shard_map/ppermute | solution.py:141
  25.1 0.4 %collective-permute-start.8 = (bf16[2,128,128]{2,1,0:T(8,128)(2,1)S(1)}, bf16[2,128,128]{2,1,0:T(8,128)(2,1)S(1)}, u32[]{:S(2)}, u32[]{:S(2)}) collective-permute-start(bf16[2,128,128]{2,1,0:T(8,128)(2,1)S(1)} %divide_convert_fusion.refs_0_), channel_id=1, source_target_pairs={{0,2},{1,3},{2,0},{3,1},{4,6},{5,7},{6,4},{7,5},{8,10},{9,11},{10,... | collective-permute-start | bytes 196616 | tf_op jit(solution)/shard_map/ppermute | solution.py:141
  25.5 2.9 %collective-permute-start.7 = (bf16[2,128,128]{2,1,0:T(8,128)(2,1)S(1)}, bf16[2,128,128]{2,1,0:T(8,128)(2,1)S(1)}, u32[]{:S(2)}, u32[]{:S(2)}) collective-permute-start(bf16[2,128,128]{2,1,0:T(8,128)(2,1)S(1)} %divide_convert_fusion.refs_0_), channel_id=1, source_target_pairs={{0,1},{1,0},{2,3},{3,2},{4,5},{5,4},{6,7},{7,6},{8,9},{9,8},{10,11... | collective-permute-start | bytes 196616 | tf_op jit(solution)/shard_map/ppermute | solution.py:141
  28.4 1.7 %collective-permute-done.9.refs_3_ = bf16[2,128,128]{2,1,0:T(8,128)(2,1)S(1)} collective-permute-done((bf16[2,128,128]{2,1,0:T(8,128)(2,1)S(1)}, bf16[2,128,128]{2,1,0:T(8,128)(2,1)S(1)}, u32[]{:S(2)}, u32[]{:S(2)}) %collective-permute-start.9) | collective-permute-done | bytes 65568 | tf_op jit(solution)/shard_map/ppermute | solution.py:141
  30.1 1.3 %collective-permute-done.8.refs_2_ = bf16[2,128,128]{2,1,0:T(8,128)(2,1)S(1)} collective-permute-done((bf16[2,128,128]{2,1,0:T(8,128)(2,1)S(1)}, bf16[2,128,128]{2,1,0:T(8,128)(2,1)S(1)}, u32[]{:S(2)}, u32[]{:S(2)}) %collective-permute-start.8) | collective-permute-done | bytes 65568 | tf_op jit(solution)/shard_map/ppermute | solution.py:141
  31.5 0.0 collective-permute-done.7.refs_1_
  31.5 0.7 %join.1 = bf16[8,128,128]{2,1,0:T(8,128)(2,1)} custom-call(bf16[2,128,128]{2,1,0:T(8,128)(2,1)S(1)} %divide_convert_fusion.refs_0_, bf16[2,128,128]{2,1,0:T(8,128)(2,1)S(1)} %collective-permute-done.7.refs_1_, bf16[2,128,128]{2,1,0:T(8,128)(2,1)S(1)} %collective-permute-done.8.refs_2_, bf16[2,128,128]{2,1,0:T(8,128)(2,1)S(1)} %collective-permute-done.9.refs_3_), custom_call_target="tpu_custom_call" | custom-call | tf_op jit(solution)/shard_map/join/pallas_call | solution.py:150
  (4 shorter events, 0.1 us)
Async XLA Ops:
  0.0 2.0 %collective-permute-start = (bf16[8,128,128]{2,1,0:T(8,128)(2,1)}, bf16[8,128,128]{2,1,0:T(8,128)(2,1)S(1)}, u32[]{:S(2)}, u32[]{:S(2)}) collective-permute-start(bf16[8,128,128]{2,1,0:T(8,128)(2,1)} %bitcast.10), channel_id=1, source_target_pairs={{0,4},{4,0},{8,12},{12,8},{16,20},{20,16},{24,28},{28,24},{1,5},{5... | collective-permute-start | bytes 786440 | tf_op jit(solution)/shard_map/ppermute | solution.py:95
  0.5 1.6 %copy-start = (bf16[1,8,128,128]{3,2,1,0:T(8,128)(2,1)S(1)}, bf16[1,8,128,128]{3,2,1,0:T(8,128)(2,1)}, u32[]{:S(2)}) copy-start(bf16[1,8,128,128]{3,2,1,0:T(8,128)(2,1)} %param.6) | copy-start | bytes 786436
  2.0 0.7 %copy-start.2 = (s32[8]{0:T(128)S(1)}, s32[8]{0:T(128)}, u32[]{:S(2)}) copy-start(s32[8]{0:T(128)} %owner_ref.3) | copy-start | bytes 100
  3.3 5.7 %collective-permute-start.1 = (bf16[2,128,128]{2,1,0:T(8,128)(2,1)S(1)}, bf16[2,128,128]{2,1,0:T(8,128)(2,1)S(1)}, u32[]{:S(2)}, u32[]{:S(2)}) collective-permute-start(bf16[2,128,128]{2,1,0:T(8,128)(2,1)S(1)} %get-tuple-element.21), channel_id=1, source_target_pairs={{0,8},{4,12},{8,0},{12,4},{16,24},{20,28},{24,16},{28,20},{1,9},{5... | collective-permute-start | bytes 196616 | tf_op jit(solution)/shard_map/ppermute | solution.py:108
  5.8 1.6 %copy-start.1 = (s32[4,8]{1,0:T(4,128)S(1)}, s32[4,8]{1,0:T(4,128)}, u32[]{:S(2)}) copy-start(s32[4,8]{1,0:T(4,128)} %screen_ref.1) | copy-start | bytes 388
  5.8 4.3 %collective-permute-start.2 = (bf16[2,128,128]{2,1,0:T(8,128)(2,1)S(1)}, bf16[2,128,128]{2,1,0:T(8,128)(2,1)S(1)}, u32[]{:S(2)}, u32[]{:S(2)}) collective-permute-start(bf16[2,128,128]{2,1,0:T(8,128)(2,1)S(1)} %get-tuple-element.22), channel_id=1, source_target_pairs={{0,16},{4,20},{8,24},{12,28},{16,0},{20,4},{24,8},{28,12},{1,17},{... | collective-permute-start | bytes 196616 | tf_op jit(solution)/shard_map/ppermute | solution.py:108
  7.3 0.7 %copy-start.3 = (f32[8]{0:T(128)S(1)}, f32[8]{0:T(128)}, u32[]{:S(2)}) copy-start(f32[8]{0:T(128)} %eps_occ_ref.1) | copy-start | bytes 100
  7.3 0.7 %copy-start.4 = (f32[128]{0:T(128)S(1)}, f32[128]{0:T(128)}, u32[]{:S(2)}) copy-start(f32[128]{0:T(128)} %param.11) | copy-start | bytes 1540
  7.4 5.2 %collective-permute-start.3 = (bf16[2,128,128]{2,1,0:T(8,128)(2,1)S(1)}, bf16[2,128,128]{2,1,0:T(8,128)(2,1)S(1)}, u32[]{:S(2)}, u32[]{:S(2)}) collective-permute-start(bf16[2,128,128]{2,1,0:T(8,128)(2,1)S(1)} %get-tuple-element.23), channel_id=1, source_target_pairs={{0,24},{4,28},{8,16},{12,20},{16,8},{20,12},{24,0},{28,4},{1,25},{... | collective-permute-start | bytes 196616 | tf_op jit(solution)/shard_map/ppermute | solution.py:108
  13.6 5.0 %collective-permute-start.4 = (bf16[2,128,128]{2,1,0:T(8,128)(2,1)S(1)}, bf16[2,128,128]{2,1,0:T(8,128)(2,1)S(1)}, u32[]{:S(2)}, u32[]{:S(2)}) collective-permute-start(bf16[2,128,128]{2,1,0:T(8,128)(2,1)S(1)} %get-tuple-element.25), channel_id=1, source_target_pairs={{0,1},{1,0},{2,3},{3,2},{4,5},{5,4},{6,7},{7,6},{8,9},{9,8},{10,11... | collective-permute-start | bytes 196616 | tf_op jit(solution)/shard_map/ppermute | solution.py:141
  15.2 6.6 %collective-permute-start.5 = (bf16[2,128,128]{2,1,0:T(8,128)(2,1)S(1)}, bf16[2,128,128]{2,1,0:T(8,128)(2,1)S(1)}, u32[]{:S(2)}, u32[]{:S(2)}) collective-permute-start(bf16[2,128,128]{2,1,0:T(8,128)(2,1)S(1)} %get-tuple-element.26), channel_id=1, source_target_pairs={{0,2},{1,3},{2,0},{3,1},{4,6},{5,7},{6,4},{7,5},{8,10},{9,11},{10,... | collective-permute-start | bytes 196616 | tf_op jit(solution)/shard_map/ppermute | solution.py:141
  17.8 6.1 %collective-permute-start.6 = (bf16[2,128,128]{2,1,0:T(8,128)(2,1)S(1)}, bf16[2,128,128]{2,1,0:T(8,128)(2,1)S(1)}, u32[]{:S(2)}, u32[]{:S(2)}) collective-permute-start(bf16[2,128,128]{2,1,0:T(8,128)(2,1)S(1)} %get-tuple-element.27), channel_id=1, source_target_pairs={{0,3},{1,2},{2,1},{3,0},{4,7},{5,6},{6,5},{7,4},{8,11},{9,10},{10,... | collective-permute-start | bytes 196616 | tf_op jit(solution)/shard_map/ppermute | solution.py:141
  23.9 6.2 %collective-permute-start.9 = (bf16[2,128,128]{2,1,0:T(8,128)(2,1)S(1)}, bf16[2,128,128]{2,1,0:T(8,128)(2,1)S(1)}, u32[]{:S(2)}, u32[]{:S(2)}) collective-permute-start(bf16[2,128,128]{2,1,0:T(8,128)(2,1)S(1)} %divide_convert_fusion.refs_0_), channel_id=1, source_target_pairs={{0,3},{1,2},{2,1},{3,0},{4,7},{5,6},{6,5},{7,4},{8,11},{9,10},{10,... | collective-permute-start | bytes 196616 | tf_op jit(solution)/shard_map/ppermute | solution.py:141
  25.1 6.4 %collective-permute-start.8 = (bf16[2,128,128]{2,1,0:T(8,128)(2,1)S(1)}, bf16[2,128,128]{2,1,0:T(8,128)(2,1)S(1)}, u32[]{:S(2)}, u32[]{:S(2)}) collective-permute-start(bf16[2,128,128]{2,1,0:T(8,128)(2,1)S(1)} %divide_convert_fusion.refs_0_), channel_id=1, source_target_pairs={{0,2},{1,3},{2,0},{3,1},{4,6},{5,7},{6,4},{7,5},{8,10},{9,11},{10,... | collective-permute-start | bytes 196616 | tf_op jit(solution)/shard_map/ppermute | solution.py:141
  25.5 6.0 %collective-permute-start.7 = (bf16[2,128,128]{2,1,0:T(8,128)(2,1)S(1)}, bf16[2,128,128]{2,1,0:T(8,128)(2,1)S(1)}, u32[]{:S(2)}, u32[]{:S(2)}) collective-permute-start(bf16[2,128,128]{2,1,0:T(8,128)(2,1)S(1)} %divide_convert_fusion.refs_0_), channel_id=1, source_target_pairs={{0,1},{1,0},{2,3},{3,2},{4,5},{5,4},{6,7},{7,6},{8,9},{9,8},{10,11... | collective-permute-start | bytes 196616 | tf_op jit(solution)/shard_map/ppermute | solution.py:141

commit v3 on v2

--- a/solution.py
+++ b/solution.py
@@ -16,30 +16,48 @@
     return i ^ k if n & (n - 1) == 0 else (i + n - k) % n
 
 
-def pack_kernel(groups, owner_ref, own_ref, mate_ref, *out_refs):
+def ring_to(i, k, n):
+    return (i + k) % n
+
+
+def ring_from(i, k, n):
+    return (i + n - k) % n
+
+
+def load_kernel(owner_hbm, own_hbm, owner_ref, own_ref, sems):
+    loads = [
+        pltpu.make_async_copy(owner_hbm, owner_ref, sems.at[0]),
+        pltpu.make_async_copy(own_hbm, own_ref, sems.at[1]),
+    ]
+    for load in loads:
+        load.start()
+    for load in loads:
+        load.wait()
+
+
+def pick(table_ref, index):
+    table = table_ref[...]
+    places = lax.broadcasted_iota(jnp.int32, table.shape, 1)
+    return jnp.sum(jnp.where(places == index, table, jnp.zeros_like(table)))
+
+
+def pack_kernel(groups, slots_ref, own_ref, mate_ref, *out_refs):
     me = lax.axis_index("tile")
     for step, out_ref in enumerate(out_refs):
         slot = 2 * hop_to(me // 2, step, groups) + me % 2
-        column = owner_ref[slot]
+        column = pick(slots_ref, slot)
         out_ref[0] = own_ref[column]
         out_ref[1] = mate_ref[column]
 
 
-def screen_kernel(flat_ref, screen_ref, owner_ref, eps_occ_ref, eps_vir_ref, out_ref, denominator_ref):
-    blocks, occ_rows = screen_ref.shape
-    share_rows, virt, _ = denominator_ref.shape
-    size = flat_ref.shape[0] // blocks
-    for block in range(blocks):
-        for k in range(occ_rows):
-            where = (pl.ds(block * size, size), pl.ds(k * virt, virt))
-            tile = flat_ref[where]
-            out_ref[where] = jnp.where(screen_ref[block, k] != 0, tile, jnp.zeros_like(tile))
+def denominator_kernel(slots_ref, eps_occ_ref, eps_vir_ref, out_ref):
+    share_rows, virt, _ = out_ref.shape
     eps_row = jnp.broadcast_to(eps_vir_ref[...], (virt, virt))
-    eps_slot = eps_occ_ref[owner_ref[lax.axis_index("tile")]]
+    eps_slot = pick(eps_occ_ref, pick(slots_ref, lax.axis_index("tile")))
     virt_pair = eps_row.T + eps_row - eps_slot
     for row in range(share_rows):
-        i = jnp.minimum(lax.axis_index("aux") * share_rows + row, occ_rows - 1)
-        denominator_ref[row] = virt_pair - eps_occ_ref[i]
+        i = jnp.minimum(lax.axis_index("aux") * share_rows + row, eps_occ_ref.shape[1] - 1)
+        out_ref[row] = virt_pair - pick(eps_occ_ref, i)
 
 
 def cycle_kernel(groups, aux_count, screened_ref, *refs):
@@ -71,12 +89,11 @@
     piece_refs, out_ref = refs[:-1], refs[-1]
     me = lax.axis_index("aux")
     for step, piece_ref in enumerate(piece_refs):
-        share = hop_from(me, step, aux_count)
+        share = ring_from(me, step, aux_count)
         out_ref[pl.ds(share * share_rows, share_rows)] = piece_ref[...]
 
 
 VMEM = pl.BlockSpec(memory_space=pltpu.VMEM)
-SMEM = pl.BlockSpec(memory_space=pltpu.SMEM)
 
 
 def room(bytes_used):
@@ -91,20 +108,31 @@
     share_rows = -(-occ_rows // aux_count)
     padded_rows = share_rows * aux_count
 
-    own = amps[0]
-    mate = lax.ppermute(own, "tile", [(t, t ^ 1) for t in range(tile_count)])
-    flat = fitted.reshape(aux_here, occ_rows * virt)
-    mate, flat = lax.optimization_barrier((mate, flat))
+    mate = lax.ppermute(amps[0], "tile", [(t, t ^ 1) for t in range(tile_count)])
+    slots, own = pl.pallas_call(
+        load_kernel,
+        name="load",
+        out_shape=[
+            jax.ShapeDtypeStruct((1, owner.shape[0]), owner.dtype),
+            jax.ShapeDtypeStruct(mate.shape, mate.dtype),
+        ],
+        in_specs=[pl.BlockSpec(memory_space=pl.ANY)] * 2,
+        out_specs=[VMEM] * 2,
+        scratch_shapes=[pltpu.SemaphoreType.DMA((2,))],
+        compiler_params=room(4 * mate.size),
+    )(owner[None, :], amps[0])
+    mate, slots, own = lax.optimization_barrier((mate, slots, own))
     tile_piece = jax.ShapeDtypeStruct((2, virt, virt), amps.dtype)
     packed = pl.pallas_call(
         functools.partial(pack_kernel, groups),
         name="pack",
         out_shape=[tile_piece] * groups,
-        in_specs=[SMEM, VMEM, VMEM],
+        in_specs=[VMEM] * 3,
         out_specs=[VMEM] * groups,
         compiler_params=room(6 * own.size),
-    )(owner, own, mate)
-    pieces = [packed[0]] + [
+    )(slots, own, mate)
+    fitted, screen, kept = lax.optimization_barrier((fitted, screen, packed[0]))
+    pieces = [kept] + [
         lax.ppermute(
             packed[step],
             "tile",
@@ -113,18 +141,19 @@
         for step in range(1, groups)
     ]
 
+    flat = fitted.reshape(aux_here, occ_rows * virt)
+    mask = screen.astype(fitted.dtype)
+    mask = jnp.repeat(mask, virt, axis=1)
+    screened = flat * jnp.repeat(mask, aux_here // screen.shape[0], axis=0)
     share = (share_rows, virt, virt)
-    screened, denominator = pl.pallas_call(
-        screen_kernel,
-        name="screen",
-        out_shape=[
-            jax.ShapeDtypeStruct(flat.shape, flat.dtype),
-            jax.ShapeDtypeStruct(share, jnp.float32),
-        ],
-        in_specs=[VMEM, SMEM, SMEM, SMEM, VMEM],
-        out_specs=[VMEM, VMEM],
-        compiler_params=room(4 * flat.size + 4 * share_rows * virt * virt),
-    )(flat, screen, owner, eps_occ, eps_vir[None, :])
+    denominator = pl.pallas_call(
+        denominator_kernel,
+        name="denominator",
+        out_shape=jax.ShapeDtypeStruct(share, jnp.float32),
+        in_specs=[VMEM] * 3,
+        out_specs=VMEM,
+        compiler_params=room(8 * share_rows * virt * virt),
+    )(slots, eps_occ[None, :], eps_vir[None, :])
     partials = pl.pallas_call(
         functools.partial(cycle_kernel, groups, aux_count),
         name="cycle",
@@ -136,17 +165,17 @@
         compiler_params=room(4 * flat.size + 8 * own.size + 8 * padded_rows * virt * virt),
     )(screened, *pieces)
 
-    def spread(value, step):
-        perm = [(z, hop_to(z, step, aux_count)) for z in range(aux_count)]
+    def spread(value, step, to):
+        perm = [(z, to(z, step, aux_count)) for z in range(aux_count)]
         return lax.ppermute(value, "aux", perm)
 
     cycle = partials[0]
     for step in range(1, aux_count):
-        cycle = cycle + spread(partials[step], step).astype(jnp.float32)
+        cycle = cycle + spread(partials[step], step, hop_to).astype(jnp.float32)
 
     divided = (cycle / denominator).astype(jnp.bfloat16)
 
-    shares = [divided] + [spread(divided, step) for step in range(1, aux_count)]
+    shares = [divided] + [spread(divided, step, ring_to) for step in range(1, aux_count)]
     joined = pl.pallas_call(
         functools.partial(join_kernel, aux_count, share_rows),
         name="join",

time: 32.4 us -> 31.3 us (0.966)
  other arithmetic: 0.05 us -> 1.42 us
  Pallas kernels: 3.32 us -> 2.22 us
  waiting for transfers between devices: 12.5 us -> 11.6 us
  local copies, waits for them, and re-layouts: 2.79 us -> 2.39 us
    mul x0 -> x1, other arithmetic: none -> 1.37 us  [on_device(): screened = flat * jnp.repeat(mask, aux_here // screen.shape[0], axis=0)]
    ppermute x6, waiting for transfers between devices: 8.94 us -> 7.65 us  [spread(): return lax.ppermute(value, 'aux', perm)]
    pallas_call x1 -> x2, Pallas kernels: 0.96 us -> 0.31 us  [the longest x1 0.27 us: on_device(): pl.pallas_call(denominator_kernel, name='denominator', out_shape=jax.Shap...]
    pallas_call x1, Pallas kernels: 0.58 us -> 0.14 us  [on_device(): pl.pallas_call(functools.partial(pack_kernel, groups), name='pack', out_s...]
    ppermute x6, starting transfers between devices: 8.9 us -> 8.5 us  [spread(): return lax.ppermute(value, 'aux', perm)]
    unnamed x11 -> x12, local copies, waits for them, and re-layouts: 2.79 us -> 2.39 us
  transfers between devices with their start and end apart: 10 -> 10, of which waited for: 7 -> 7; matrix products, arithmetic and copies ran while one was open for 5% -> 5% of each run, Pallas kernels for 3% -> 1%
where the time goes in v3:
time: 31.3 us; the launch traced here: 31 us
  starting transfers between devices  13.4 us (43%)
  waiting for transfers between devices  11.6 us (37%)
  local copies, waits for them, and re-layouts  2.39 us (8%)
  Pallas kernels  2.22 us (7%)
  other arithmetic  1.42 us (5%)
    ppermute x6, starting transfers between devices, spread(): return lax.ppermute(value, 'aux', perm)  8.5 us
    ppermute x6, waiting for transfers between devices, spread(): return lax.ppermute(value, 'aux', perm)  7.65 us
    ppermute x3, starting transfers between devices, on_device(): lax.ppermute(packed[step], 'tile', [(t, 2 * hop_to(t // 2, step, groups)...  4.37 us
    ppermute x3, waiting for transfers between devices, on_device(): lax.ppermute(packed[step], 'tile', [(t, 2 * hop_to(t // 2, step, groups)...  3.7 us
    unnamed x12, local copies, waits for them, and re-layouts  2.39 us
    mul x1, other arithmetic, on_device(): screened = flat * jnp.repeat(mask, aux_here // screen.shape[0], axis=0)  1.37 us
    pallas_call x1, Pallas kernels, on_device(): pl.pallas_call(functools.partial(cycle_kernel, groups, aux_count), name='...  1.05 us
    pallas_call x1, Pallas kernels, on_device(): pl.pallas_call(functools.partial(join_kernel, aux_count, share_rows), nam...  0.72 us
  transfers between devices with their start and end apart: 10, of which 7 were waited for; matrix products, arithmetic and copies ran while one was open for 5% of the time, Pallas kernels for 1%

profile of v3, /device:TPU:0, one launch (start us, length us, event | category | flops | bytes accessed | tf_op | source)
XLA Modules:
  0.0 31.0 jit_solution(6942930734861734187)
XLA Ops:
  0.0 0.0 copy-start.1
  0.0 0.5 %collective-permute-start = (bf16[8,128,128]{2,1,0:T(8,128)(2,1)}, bf16[8,128,128]{2,1,0:T(8,128)(2,1)S(1)}, u32[]{:S(2)}, u32[]{:S(2)}) collective-permute-start(bf16[8,128,128]{2,1,0:T(8,128)(2,1)} %bitcast.17), channel_id=1, source_target_pairs={{0,4},{4,0},{8,12},{12,8},{16,20},{20,16},{24,28},{28,24},{1,5},{5... | collective-permute-start | bytes 786440 | tf_op jit(solution)/shard_map/ppermute | solution.py:111
  0.5 0.2 copy-done.1
  0.7 0.9 %copy-done = bf16[1,8,128,128]{3,2,1,0:T(8,128)(2,1)S(1)} copy-done((bf16[1,8,128,128]{3,2,1,0:T(8,128)(2,1)S(1)}, bf16[1,8,128,128]{3,2,1,0:T(8,128)(2,1)}, u32[]{:S(2)}) %copy-start) | copy-done | bytes 262168
  1.7 0.2 collective-permute-done.mate_ref
  1.9 0.1 pack.1
  2.0 0.5 %copy-done.4 = s32[4,8]{1,0:T(4,128)S(1)} copy-done((s32[4,8]{1,0:T(4,128)S(1)}, s32[4,8]{1,0:T(4,128)}, u32[]{:S(2)}) %copy-start.4) | copy-done | bytes 152
  2.6 2.8 %collective-permute-start.1 = (bf16[2,128,128]{2,1,0:T(8,128)(2,1)S(1)}, bf16[2,128,128]{2,1,0:T(8,128)(2,1)S(1)}, u32[]{:S(2)}, u32[]{:S(2)}) collective-permute-start(bf16[2,128,128]{2,1,0:T(8,128)(2,1)S(1)} %get-tuple-element.30), channel_id=1, source_target_pairs={{0,8},{4,12},{8,0},{12,4},{16,24},{20,28},{24,16},{28,20},{1,9},{5... | collective-permute-start | bytes 196616 | tf_op jit(solution)/shard_map/ppermute | solution.py:136
  5.4 1.5 %collective-permute-start.2 = (bf16[2,128,128]{2,1,0:T(8,128)(2,1)S(1)}, bf16[2,128,128]{2,1,0:T(8,128)(2,1)S(1)}, u32[]{:S(2)}, u32[]{:S(2)}) collective-permute-start(bf16[2,128,128]{2,1,0:T(8,128)(2,1)S(1)} %get-tuple-element.31), channel_id=1, source_target_pairs={{0,16},{4,20},{8,24},{12,28},{16,0},{20,4},{24,8},{28,12},{1,17},{... | collective-permute-start | bytes 196616 | tf_op jit(solution)/shard_map/ppermute | solution.py:136
  6.9 0.0 collective-permute-start.3
  6.9 0.1 broadcast_bitcast_fusion
  7.0 1.4 %bitcast_multiply_fusion.screened_ref = bf16[512,1024]{1,0:T(8,128)(2,1)S(1)} fusion(bf16[64,8,8,128]{3,2,1,0:T(8,128)(2,1)} %bitcast.22, bf16[4,1024]{1,0:T(4,128)(2,1)S(1)} %bitcast.23), kind=kLoop, calls=%fused_computation | loop fusion | flops 524288 | bytes 2105344 | tf_op jit(solution)/shard_map/mul | solution.py:147
  8.4 0.0 collective-permute-done.1.refs_1_
  8.4 1.3 %collective-permute-done.2.refs_2_ = bf16[2,128,128]{2,1,0:T(8,128)(2,1)S(1)} collective-permute-done((bf16[2,128,128]{2,1,0:T(8,128)(2,1)S(1)}, bf16[2,128,128]{2,1,0:T(8,128)(2,1)S(1)}, u32[]{:S(2)}, u32[]{:S(2)}) %collective-permute-start.2) | collective-permute-done | bytes 65568 | tf_op jit(solution)/shard_map/ppermute | solution.py:136
  9.7 2.4 %collective-permute-done.3.refs_3_ = bf16[2,128,128]{2,1,0:T(8,128)(2,1)S(1)} collective-permute-done((bf16[2,128,128]{2,1,0:T(8,128)(2,1)S(1)}, bf16[2,128,128]{2,1,0:T(8,128)(2,1)S(1)}, u32[]{:S(2)}, u32[]{:S(2)}) %collective-permute-start.3) | collective-permute-done | bytes 65568 | tf_op jit(solution)/shard_map/ppermute | solution.py:136
  12.1 1.1 %cycle.1 = (f32[2,128,128]{2,1,0:T(8,128)S(1)}, bf16[2,128,128]{2,1,0:T(8,128)(2,1)S(1)}, bf16[2,128,128]{2,1,0:T(8,128)(2,1)S(1)}, bf16[2,128,128]{2,1,0:T(8,128)(2,1)S(1)}) custom-call(bf16[512,1024]{1,0:T(8,128)(2,1)S(1)} %bitcast_multiply_fusion.screened_ref, bf16[2,128,128]{2,1,0:T(8,128)(2,1)S(1)} %get-tuple-element.29.refs_0_, ...), custom_call_target="tpu_custom_call" | custom-call | tf_op jit(solution)/shard_map/cycle/pallas_call | solution.py:157
  13.1 1.6 %collective-permute-start.4 = (bf16[2,128,128]{2,1,0:T(8,128)(2,1)S(1)}, bf16[2,128,128]{2,1,0:T(8,128)(2,1)S(1)}, u32[]{:S(2)}, u32[]{:S(2)}) collective-permute-start(bf16[2,128,128]{2,1,0:T(8,128)(2,1)S(1)} %get-tuple-element.34), channel_id=1, source_target_pairs={{0,1},{1,0},{2,3},{3,2},{4,5},{5,4},{6,7},{7,6},{8,9},{9,8},{10,11... | collective-permute-start | bytes 196616 | tf_op jit(solution)/shard_map/ppermute | solution.py:170
  14.8 2.6 %collective-permute-start.5 = (bf16[2,128,128]{2,1,0:T(8,128)(2,1)S(1)}, bf16[2,128,128]{2,1,0:T(8,128)(2,1)S(1)}, u32[]{:S(2)}, u32[]{:S(2)}) collective-permute-start(bf16[2,128,128]{2,1,0:T(8,128)(2,1)S(1)} %get-tuple-element.35), channel_id=1, source_target_pairs={{0,2},{1,3},{2,0},{3,1},{4,6},{5,7},{6,4},{7,5},{8,10},{9,11},{10,... | collective-permute-start | bytes 196616 | tf_op jit(solution)/shard_map/ppermute | solution.py:170
  17.4 0.2 collective-permute-start.6
  17.6 0.7 %copy-done.2 = f32[8]{0:T(128)S(1)} copy-done((f32[8]{0:T(128)S(1)}, f32[8]{0:T(128)}, u32[]{:S(2)}) %copy-start.2) | copy-done | bytes 56
  18.3 0.0 copy-done.3
  18.3 0.3 denominator.1
  18.5 0.0 collective-permute-done.4
  18.6 2.8 %collective-permute-done.5 = bf16[2,128,128]{2,1,0:T(8,128)(2,1)S(1)} collective-permute-done((bf16[2,128,128]{2,1,0:T(8,128)(2,1)S(1)}, bf16[2,128,128]{2,1,0:T(8,128)(2,1)S(1)}, u32[]{:S(2)}, u32[]{:S(2)}) %collective-permute-start.5) | collective-permute-done | bytes 65568 | tf_op jit(solution)/shard_map/ppermute | solution.py:170
  21.4 2.1 %collective-permute-done.6 = bf16[2,128,128]{2,1,0:T(8,128)(2,1)S(1)} collective-permute-done((bf16[2,128,128]{2,1,0:T(8,128)(2,1)S(1)}, bf16[2,128,128]{2,1,0:T(8,128)(2,1)S(1)}, u32[]{:S(2)}, u32[]{:S(2)}) %collective-permute-start.6) | collective-permute-done | bytes 65568 | tf_op jit(solution)/shard_map/ppermute | solution.py:170
  23.5 0.1 collective-permute-start.7
  23.6 1.4 %collective-permute-start.8 = (bf16[2,128,128]{2,1,0:T(8,128)(2,1)S(1)}, bf16[2,128,128]{2,1,0:T(8,128)(2,1)S(1)}, u32[]{:S(2)}, u32[]{:S(2)}) collective-permute-start(bf16[2,128,128]{2,1,0:T(8,128)(2,1)S(1)} %divide_convert_fusion.refs_0_), channel_id=1, source_target_pairs={{0,2},{1,3},{2,0},{3,1},{4,6},{5,7},{6,4},{7,5},{8,10},{9,11},{10,... | collective-permute-start | bytes 196616 | tf_op jit(solution)/shard_map/ppermute | solution.py:170
  24.9 2.6 %collective-permute-start.9 = (bf16[2,128,128]{2,1,0:T(8,128)(2,1)S(1)}, bf16[2,128,128]{2,1,0:T(8,128)(2,1)S(1)}, u32[]{:S(2)}, u32[]{:S(2)}) collective-permute-start(bf16[2,128,128]{2,1,0:T(8,128)(2,1)S(1)} %divide_convert_fusion.refs_0_), channel_id=1, source_target_pairs={{0,3},{1,0},{2,1},{3,2},{4,7},{5,4},{6,5},{7,6},{8,11},{9,8},{10,9... | collective-permute-start | bytes 196616 | tf_op jit(solution)/shard_map/ppermute | solution.py:170
  27.5 2.1 %collective-permute-done.7.refs_1_ = bf16[2,128,128]{2,1,0:T(8,128)(2,1)S(1)} collective-permute-done((bf16[2,128,128]{2,1,0:T(8,128)(2,1)S(1)}, bf16[2,128,128]{2,1,0:T(8,128)(2,1)S(1)}, u32[]{:S(2)}, u32[]{:S(2)}) %collective-permute-start.7) | collective-permute-done | bytes 65568 | tf_op jit(solution)/shard_map/ppermute | solution.py:170
  29.6 0.0 collective-permute-done.8.refs_2_
  29.6 0.7 %collective-permute-done.9.refs_3_ = bf16[2,128,128]{2,1,0:T(8,128)(2,1)S(1)} collective-permute-done((bf16[2,128,128]{2,1,0:T(8,128)(2,1)S(1)}, bf16[2,128,128]{2,1,0:T(8,128)(2,1)S(1)}, u32[]{:S(2)}, u32[]{:S(2)}) %collective-permute-start.9) | collective-permute-done | bytes 65568 | tf_op jit(solution)/shard_map/ppermute | solution.py:170
  30.3 0.7 %join.1 = bf16[8,128,128]{2,1,0:T(8,128)(2,1)} custom-call(bf16[2,128,128]{2,1,0:T(8,128)(2,1)S(1)} %divide_convert_fusion.refs_0_, bf16[2,128,128]{2,1,0:T(8,128)(2,1)S(1)} %collective-permute-done.7.refs_1_, bf16[2,128,128]{2,1,0:T(8,128)(2,1)S(1)} %collective-permute-done.8.refs_2_, bf16[2,128,128]{2,1,0:T(8,128)(2,1)S(1)} %collective-permute-done.9.refs_3_), custom_call_target="tpu_custom_call" | custom-call | tf_op jit(solution)/shard_map/join/pallas_call | solution.py:179
  (8 shorter events, 0.1 us)
Async XLA Ops:
  0.0 0.7 %copy-start.1 = (s32[8]{0:T(128)S(1)}, s32[8]{0:T(128)}, u32[]{:S(2)}) copy-start(s32[8]{0:T(128)} %param.9) | copy-start | bytes 100
  0.0 1.9 %collective-permute-start = (bf16[8,128,128]{2,1,0:T(8,128)(2,1)}, bf16[8,128,128]{2,1,0:T(8,128)(2,1)S(1)}, u32[]{:S(2)}, u32[]{:S(2)}) collective-permute-start(bf16[8,128,128]{2,1,0:T(8,128)(2,1)} %bitcast.17), channel_id=1, source_target_pairs={{0,4},{4,0},{8,12},{12,8},{16,20},{20,16},{24,28},{28,24},{1,5},{5... | collective-permute-start | bytes 786440 | tf_op jit(solution)/shard_map/ppermute | solution.py:111
  0.7 0.9 %copy-start = (bf16[1,8,128,128]{3,2,1,0:T(8,128)(2,1)S(1)}, bf16[1,8,128,128]{3,2,1,0:T(8,128)(2,1)}, u32[]{:S(2)}) copy-start(bf16[1,8,128,128]{3,2,1,0:T(8,128)(2,1)} %param.6) | copy-start | bytes 786436
  1.9 0.7 %copy-start.4 = (s32[4,8]{1,0:T(4,128)S(1)}, s32[4,8]{1,0:T(4,128)}, u32[]{:S(2)}) copy-start(s32[4,8]{1,0:T(4,128)} %param.8) | copy-start | bytes 388
  2.6 5.8 %collective-permute-start.1 = (bf16[2,128,128]{2,1,0:T(8,128)(2,1)S(1)}, bf16[2,128,128]{2,1,0:T(8,128)(2,1)S(1)}, u32[]{:S(2)}, u32[]{:S(2)}) collective-permute-start(bf16[2,128,128]{2,1,0:T(8,128)(2,1)S(1)} %get-tuple-element.30), channel_id=1, source_target_pairs={{0,8},{4,12},{8,0},{12,4},{16,24},{20,28},{24,16},{28,20},{1,9},{5... | collective-permute-start | bytes 196616 | tf_op jit(solution)/shard_map/ppermute | solution.py:136
  5.4 4.3 %collective-permute-start.2 = (bf16[2,128,128]{2,1,0:T(8,128)(2,1)S(1)}, bf16[2,128,128]{2,1,0:T(8,128)(2,1)S(1)}, u32[]{:S(2)}, u32[]{:S(2)}) collective-permute-start(bf16[2,128,128]{2,1,0:T(8,128)(2,1)S(1)} %get-tuple-element.31), channel_id=1, source_target_pairs={{0,16},{4,20},{8,24},{12,28},{16,0},{20,4},{24,8},{28,12},{1,17},{... | collective-permute-start | bytes 196616 | tf_op jit(solution)/shard_map/ppermute | solution.py:136
  6.9 5.2 %collective-permute-start.3 = (bf16[2,128,128]{2,1,0:T(8,128)(2,1)S(1)}, bf16[2,128,128]{2,1,0:T(8,128)(2,1)S(1)}, u32[]{:S(2)}, u32[]{:S(2)}) collective-permute-start(bf16[2,128,128]{2,1,0:T(8,128)(2,1)S(1)} %get-tuple-element.32), channel_id=1, source_target_pairs={{0,24},{4,28},{8,16},{12,20},{16,8},{20,12},{24,0},{28,4},{1,25},{... | collective-permute-start | bytes 196616 | tf_op jit(solution)/shard_map/ppermute | solution.py:136
  13.1 5.4 %collective-permute-start.4 = (bf16[2,128,128]{2,1,0:T(8,128)(2,1)S(1)}, bf16[2,128,128]{2,1,0:T(8,128)(2,1)S(1)}, u32[]{:S(2)}, u32[]{:S(2)}) collective-permute-start(bf16[2,128,128]{2,1,0:T(8,128)(2,1)S(1)} %get-tuple-element.34), channel_id=1, source_target_pairs={{0,1},{1,0},{2,3},{3,2},{4,5},{5,4},{6,7},{7,6},{8,9},{9,8},{10,11... | collective-permute-start | bytes 196616 | tf_op jit(solution)/shard_map/ppermute | solution.py:170
  14.8 6.6 %collective-permute-start.5 = (bf16[2,128,128]{2,1,0:T(8,128)(2,1)S(1)}, bf16[2,128,128]{2,1,0:T(8,128)(2,1)S(1)}, u32[]{:S(2)}, u32[]{:S(2)}) collective-permute-start(bf16[2,128,128]{2,1,0:T(8,128)(2,1)S(1)} %get-tuple-element.35), channel_id=1, source_target_pairs={{0,2},{1,3},{2,0},{3,1},{4,6},{5,7},{6,4},{7,5},{8,10},{9,11},{10,... | collective-permute-start | bytes 196616 | tf_op jit(solution)/shard_map/ppermute | solution.py:170
  17.4 6.1 %collective-permute-start.6 = (bf16[2,128,128]{2,1,0:T(8,128)(2,1)S(1)}, bf16[2,128,128]{2,1,0:T(8,128)(2,1)S(1)}, u32[]{:S(2)}, u32[]{:S(2)}) collective-permute-start(bf16[2,128,128]{2,1,0:T(8,128)(2,1)S(1)} %get-tuple-element.36), channel_id=1, source_target_pairs={{0,3},{1,2},{2,1},{3,0},{4,7},{5,6},{6,5},{7,4},{8,11},{9,10},{10,... | collective-permute-start | bytes 196616 | tf_op jit(solution)/shard_map/ppermute | solution.py:170
  17.6 0.7 %copy-start.2 = (f32[8]{0:T(128)S(1)}, f32[8]{0:T(128)}, u32[]{:S(2)}) copy-start(f32[8]{0:T(128)} %param.10) | copy-start | bytes 100
  17.6 0.7 %copy-start.3 = (f32[128]{0:T(128)S(1)}, f32[128]{0:T(128)}, u32[]{:S(2)}) copy-start(f32[128]{0:T(128)} %param.11) | copy-start | bytes 1540
  23.5 6.1 %collective-permute-start.7 = (bf16[2,128,128]{2,1,0:T(8,128)(2,1)S(1)}, bf16[2,128,128]{2,1,0:T(8,128)(2,1)S(1)}, u32[]{:S(2)}, u32[]{:S(2)}) collective-permute-start(bf16[2,128,128]{2,1,0:T(8,128)(2,1)S(1)} %divide_convert_fusion.refs_0_), channel_id=1, source_target_pairs={{0,1},{1,2},{2,3},{3,0},{4,5},{5,6},{6,7},{7,4},{8,9},{9,10},{10,1... | collective-permute-start | bytes 196616 | tf_op jit(solution)/shard_map/ppermute | solution.py:170
  23.6 6.1 %collective-permute-start.8 = (bf16[2,128,128]{2,1,0:T(8,128)(2,1)S(1)}, bf16[2,128,128]{2,1,0:T(8,128)(2,1)S(1)}, u32[]{:S(2)}, u32[]{:S(2)}) collective-permute-start(bf16[2,128,128]{2,1,0:T(8,128)(2,1)S(1)} %divide_convert_fusion.refs_0_), channel_id=1, source_target_pairs={{0,2},{1,3},{2,0},{3,1},{4,6},{5,7},{6,4},{7,5},{8,10},{9,11},{10,... | collective-permute-start | bytes 196616 | tf_op jit(solution)/shard_map/ppermute | solution.py:170
  24.9 5.4 %collective-permute-start.9 = (bf16[2,128,128]{2,1,0:T(8,128)(2,1)S(1)}, bf16[2,128,128]{2,1,0:T(8,128)(2,1)S(1)}, u32[]{:S(2)}, u32[]{:S(2)}) collective-permute-start(bf16[2,128,128]{2,1,0:T(8,128)(2,1)S(1)} %divide_convert_fusion.refs_0_), channel_id=1, source_target_pairs={{0,3},{1,0},{2,1},{3,2},{4,7},{5,4},{6,5},{7,6},{8,11},{9,8},{10,9... | collective-permute-start | bytes 196616 | tf_op jit(solution)/shard_map/ppermute | solution.py:170

commit v4 on v3

--- a/solution.py
+++ b/solution.py
@@ -46,8 +46,8 @@
     for step, out_ref in enumerate(out_refs):
         slot = 2 * hop_to(me // 2, step, groups) + me % 2
         column = pick(slots_ref, slot)
-        out_ref[0] = own_ref[column]
-        out_ref[1] = mate_ref[column]
+        out_ref[me % 2] = own_ref[column]
+        out_ref[1 - me % 2] = mate_ref[column]
 
 
 def denominator_kernel(slots_ref, eps_occ_ref, eps_vir_ref, out_ref):
@@ -60,29 +60,44 @@
         out_ref[row] = virt_pair - pick(eps_occ_ref, i)
 
 
-def cycle_kernel(groups, aux_count, screened_ref, *refs):
-    piece_refs, out_refs, amps_ref = refs[:groups], refs[groups:-1], refs[-1]
-    me = lax.axis_index("tile")
-    occ_rows, virt = screened_ref.shape[1] // amps_ref.shape[1], amps_ref.shape[1]
-    for step, piece_ref in enumerate(piece_refs):
-        group = hop_from(me // 2, step, groups)
-        for part in range(2):
-            k = 2 * group + (me + part) % 2
-            amps_ref[pl.ds(pl.multiple_of(k * virt, virt), virt), :] = piece_ref[part]
-    inter = jnp.dot(
-        screened_ref[...], amps_ref[...], preferred_element_type=jnp.float32
-    ).astype(jnp.bfloat16)
-    share_rows = out_refs[0].shape[0]
-    last = (occ_rows - share_rows) * virt
-    for step, out_ref in enumerate(out_refs):
-        share = hop_to(lax.axis_index("aux"), step, aux_count)
-        start = jnp.minimum(share * share_rows * virt, last)
-        columns = screened_ref[:, pl.ds(pl.multiple_of(start, virt), share_rows * virt)]
-        flipped = lax.dot_general(
-            inter, columns, (((0,), (0,)), ((), ())), preferred_element_type=jnp.float32
-        )
-        for row in range(share_rows):
-            out_ref[row] = flipped[:, row * virt : (row + 1) * virt].T.astype(out_ref.dtype)
+def inter_term(groups, step, screened_ref, piece_ref):
+    pair, virt, _ = piece_ref.shape
+    group = hop_from(lax.axis_index("tile") // 2, step, groups)
+    start = pl.multiple_of(group * pair * virt, pair * virt)
+    columns = screened_ref[:, pl.ds(start, pair * virt)]
+    piece = piece_ref[...].reshape(pair * virt, virt)
+    return jnp.dot(columns, piece, preferred_element_type=jnp.float32)
+
+
+def own_kernel(groups, screened_ref, piece_ref, out_ref):
+    out_ref[...] = inter_term(groups, 0, screened_ref, piece_ref)
+
+
+def cycle_share(aux_count, step, inter, screened_ref, out_ref):
+    share_rows, virt, _ = out_ref.shape
+    share = hop_to(lax.axis_index("aux"), step, aux_count)
+    start = jnp.minimum(share * share_rows * virt, screened_ref.shape[1] - share_rows * virt)
+    columns = screened_ref[:, pl.ds(pl.multiple_of(start, virt), share_rows * virt)]
+    flipped = lax.dot_general(
+        inter, columns, (((0,), (0,)), ((), ())), preferred_element_type=jnp.float32
+    )
+    for row in range(share_rows):
+        out_ref[row] = flipped[:, row * virt : (row + 1) * virt].T.astype(out_ref.dtype)
+
+
+def others_kernel(groups, aux_count, own_ref, screened_ref, *refs):
+    piece_refs, inter_ref, out_refs = refs[: groups - 1], refs[groups - 1], refs[groups:]
+    total = own_ref[...]
+    for step, piece_ref in enumerate(piece_refs, 1):
+        total += inter_term(groups, step, screened_ref, piece_ref)
+    inter = total.astype(inter_ref.dtype)
+    inter_ref[...] = inter
+    for step, out_ref in enumerate(out_refs, 1):
+        cycle_share(aux_count, step, inter, screened_ref, out_ref)
+
+
+def kept_kernel(aux_count, inter_ref, screened_ref, out_ref):
+    cycle_share(aux_count, 0, inter_ref[...], screened_ref, out_ref)
 
 
 def join_kernel(aux_count, share_rows, *refs):
@@ -154,24 +169,40 @@
         out_specs=VMEM,
         compiler_params=room(8 * share_rows * virt * virt),
     )(slots, eps_occ[None, :], eps_vir[None, :])
-    partials = pl.pallas_call(
-        functools.partial(cycle_kernel, groups, aux_count),
-        name="cycle",
-        out_shape=[jax.ShapeDtypeStruct(share, jnp.float32)]
-        + [jax.ShapeDtypeStruct(share, jnp.bfloat16)] * (aux_count - 1),
+    inter_shape = jax.ShapeDtypeStruct((aux_here, virt), jnp.bfloat16)
+    grant = room(2 * flat.size + 8 * inter_shape.size + 8 * own.size + 8 * padded_rows * virt * virt)
+    inter_own = pl.pallas_call(
+        functools.partial(own_kernel, groups),
+        name="own",
+        out_shape=jax.ShapeDtypeStruct(inter_shape.shape, jnp.float32),
+        in_specs=[VMEM] * 2,
+        out_specs=VMEM,
+        compiler_params=grant,
+    )(screened, pieces[0])
+    inter, *sent = pl.pallas_call(
+        functools.partial(others_kernel, groups, aux_count),
+        name="others",
+        out_shape=[inter_shape] + [jax.ShapeDtypeStruct(share, jnp.bfloat16)] * (aux_count - 1),
         in_specs=[VMEM] * (1 + groups),
         out_specs=[VMEM] * aux_count,
-        scratch_shapes=[pltpu.VMEM((occ_rows * virt, virt), amps.dtype)],
-        compiler_params=room(4 * flat.size + 8 * own.size + 8 * padded_rows * virt * virt),
-    )(screened, *pieces)
+        compiler_params=grant,
+    )(inter_own, screened, *pieces[1:])
+    kept_rows = pl.pallas_call(
+        functools.partial(kept_kernel, aux_count),
+        name="kept",
+        out_shape=jax.ShapeDtypeStruct(share, jnp.float32),
+        in_specs=[VMEM] * 2,
+        out_specs=VMEM,
+        compiler_params=grant,
+    )(inter, screened)
 
     def spread(value, step, to):
         perm = [(z, to(z, step, aux_count)) for z in range(aux_count)]
         return lax.ppermute(value, "aux", perm)
 
-    cycle = partials[0]
-    for step in range(1, aux_count):
-        cycle = cycle + spread(partials[step], step, hop_to).astype(jnp.float32)
+    cycle = kept_rows
+    for step, partial in enumerate(sent, 1):
+        cycle = cycle + spread(partial, step, hop_to).astype(jnp.float32)
 
     divided = (cycle / denominator).astype(jnp.bfloat16)
 

time: 31.3 us -> 31.1 us (level)
  waiting for transfers between devices: 11.6 us -> 11 us
    pallas_call x1 -> x3, Pallas kernels: 1.05 us -> 1.36 us  [the longest x1 0.85 us: on_device(): pl.pallas_call(functools.partial(others_kernel, groups, aux_count), name=...]
  transfers between devices with their start and end apart: 10 -> 10, of which waited for: 7 -> 7; matrix products, arithmetic and copies ran while one was open for 5% -> 5% of each run, Pallas kernels for 1% -> 3%
where the time goes in v4:
time: 31.1 us; the launch traced here: 30.8 us
  starting transfers between devices  13.4 us (43%)
  waiting for transfers between devices  11 us (35%)
  Pallas kernels  2.53 us (8%)
  local copies, waits for them, and re-layouts  2.39 us (8%)
  other arithmetic  1.43 us (5%)
    ppermute x6, starting transfers between devices, spread(): return lax.ppermute(value, 'aux', perm)  8.5 us
    ppermute x6, waiting for transfers between devices, spread(): return lax.ppermute(value, 'aux', perm)  7.35 us
    ppermute x3, starting transfers between devices, on_device(): lax.ppermute(packed[step], 'tile', [(t, 2 * hop_to(t // 2, step, groups)...  4.37 us
    ppermute x3, waiting for transfers between devices, on_device(): lax.ppermute(packed[step], 'tile', [(t, 2 * hop_to(t // 2, step, groups)...  3.47 us
    unnamed x12, local copies, waits for them, and re-layouts  2.39 us
    mul x1, other arithmetic, on_device(): screened = flat * jnp.repeat(mask, aux_here // screen.shape[0], axis=0)  1.37 us
    pallas_call x1, Pallas kernels, on_device(): pl.pallas_call(functools.partial(others_kernel, groups, aux_count), name=...  0.85 us
    pallas_call x1, Pallas kernels, on_device(): pl.pallas_call(functools.partial(join_kernel, aux_count, share_rows), nam...  0.72 us
  transfers between devices with their start and end apart: 10, of which 7 were waited for; matrix products, arithmetic and copies ran while one was open for 5% of the time, Pallas kernels for 3%

profile of v4, /device:TPU:0, one launch (start us, length us, event | category | flops | bytes accessed | tf_op | source)
XLA Modules:
  0.0 30.8 jit_solution(1244744511343843527)
XLA Ops:
  0.0 0.5 %collective-permute-start = (bf16[8,128,128]{2,1,0:T(8,128)(2,1)}, bf16[8,128,128]{2,1,0:T(8,128)(2,1)S(1)}, u32[]{:S(2)}, u32[]{:S(2)}) collective-permute-start(bf16[8,128,128]{2,1,0:T(8,128)(2,1)} %bitcast.17), channel_id=1, source_target_pairs={{0,4},{4,0},{8,12},{12,8},{16,20},{20,16},{24,28},{28,24},{1,5},{5... | collective-permute-start | bytes 786440 | tf_op jit(solution)/shard_map/ppermute | solution.py:126
  0.5 0.2 copy-done.1
  0.7 0.9 %copy-done = bf16[1,8,128,128]{3,2,1,0:T(8,128)(2,1)S(1)} copy-done((bf16[1,8,128,128]{3,2,1,0:T(8,128)(2,1)S(1)}, bf16[1,8,128,128]{3,2,1,0:T(8,128)(2,1)}, u32[]{:S(2)}) %copy-start) | copy-done | bytes 262168
  1.7 0.2 collective-permute-done.mate_ref
  1.9 0.1 pack.1
  2.0 0.5 %copy-done.4 = s32[4,8]{1,0:T(4,128)S(1)} copy-done((s32[4,8]{1,0:T(4,128)S(1)}, s32[4,8]{1,0:T(4,128)}, u32[]{:S(2)}) %copy-start.4) | copy-done | bytes 152
  2.6 2.8 %collective-permute-start.1 = (bf16[2,128,128]{2,1,0:T(8,128)(2,1)S(1)}, bf16[2,128,128]{2,1,0:T(8,128)(2,1)S(1)}, u32[]{:S(2)}, u32[]{:S(2)}) collective-permute-start(bf16[2,128,128]{2,1,0:T(8,128)(2,1)S(1)} %get-tuple-element.30), channel_id=1, source_target_pairs={{0,8},{4,12},{8,0},{12,4},{16,24},{20,28},{24,16},{28,20},{1,9},{5... | collective-permute-start | bytes 196616 | tf_op jit(solution)/shard_map/ppermute | solution.py:151
  5.4 1.5 %collective-permute-start.2 = (bf16[2,128,128]{2,1,0:T(8,128)(2,1)S(1)}, bf16[2,128,128]{2,1,0:T(8,128)(2,1)S(1)}, u32[]{:S(2)}, u32[]{:S(2)}) collective-permute-start(bf16[2,128,128]{2,1,0:T(8,128)(2,1)S(1)} %get-tuple-element.31), channel_id=1, source_target_pairs={{0,16},{4,20},{8,24},{12,28},{16,0},{20,4},{24,8},{28,12},{1,17},{... | collective-permute-start | bytes 196616 | tf_op jit(solution)/shard_map/ppermute | solution.py:151
  6.9 0.0 collective-permute-start.3
  6.9 0.1 broadcast_bitcast_fusion
  7.0 1.4 %bitcast_multiply_fusion.screened_ref = bf16[512,1024]{1,0:T(8,128)(2,1)S(1)} fusion(bf16[64,8,8,128]{3,2,1,0:T(8,128)(2,1)} %bitcast.22, bf16[4,1024]{1,0:T(4,128)(2,1)S(1)} %bitcast.23), kind=kLoop, calls=%fused_computation | loop fusion | flops 524288 | bytes 2105344 | tf_op jit(solution)/shard_map/mul | solution.py:162
  8.4 0.2 own.1.own_ref
  8.6 1.1 %collective-permute-done.2.refs_1_ = bf16[2,128,128]{2,1,0:T(8,128)(2,1)S(1)} collective-permute-done((bf16[2,128,128]{2,1,0:T(8,128)(2,1)S(1)}, bf16[2,128,128]{2,1,0:T(8,128)(2,1)S(1)}, u32[]{:S(2)}, u32[]{:S(2)}) %collective-permute-start.2) | collective-permute-done | bytes 65568 | tf_op jit(solution)/shard_map/ppermute | solution.py:151
  9.7 2.4 %collective-permute-done.3.refs_2_ = bf16[2,128,128]{2,1,0:T(8,128)(2,1)S(1)} collective-permute-done((bf16[2,128,128]{2,1,0:T(8,128)(2,1)S(1)}, bf16[2,128,128]{2,1,0:T(8,128)(2,1)S(1)}, u32[]{:S(2)}, u32[]{:S(2)}) %collective-permute-start.3) | collective-permute-done | bytes 65568 | tf_op jit(solution)/shard_map/ppermute | solution.py:151
  12.1 0.8 %others.1 = (bf16[512,128]{1,0:T(8,128)(2,1)S(1)}, bf16[2,128,128]{2,1,0:T(8,128)(2,1)S(1)}, bf16[2,128,128]{2,1,0:T(8,128)(2,1)S(1)}, bf16[2,128,128]{2,1,0:T(8,128)(2,1)S(1)}) custom-call(f32[512,128]{1,0:T(8,128)S(1)} %own.1.own_ref, bf16[512,1024]{1,0:T(8,128)(2,1)S(1)} %bitcast_multiply_fusion.screened_ref, ...), custom_call_target="tpu_custom_call" | custom-call | tf_op jit(solution)/shard_map/others/pallas_call | solution.py:182
  12.9 1.6 %collective-permute-start.4 = (bf16[2,128,128]{2,1,0:T(8,128)(2,1)S(1)}, bf16[2,128,128]{2,1,0:T(8,128)(2,1)S(1)}, u32[]{:S(2)}, u32[]{:S(2)}) collective-permute-start(bf16[2,128,128]{2,1,0:T(8,128)(2,1)S(1)} %get-tuple-element.34), channel_id=1, source_target_pairs={{0,1},{1,0},{2,3},{3,2},{4,5},{5,4},{6,7},{7,6},{8,9},{9,8},{10,11... | collective-permute-start | bytes 196616 | tf_op jit(solution)/shard_map/ppermute | solution.py:201
  14.6 2.6 %collective-permute-start.5 = (bf16[2,128,128]{2,1,0:T(8,128)(2,1)S(1)}, bf16[2,128,128]{2,1,0:T(8,128)(2,1)S(1)}, u32[]{:S(2)}, u32[]{:S(2)}) collective-permute-start(bf16[2,128,128]{2,1,0:T(8,128)(2,1)S(1)} %get-tuple-element.35), channel_id=1, source_target_pairs={{0,2},{1,3},{2,0},{3,1},{4,6},{5,7},{6,4},{7,5},{8,10},{9,11},{10,... | collective-permute-start | bytes 196616 | tf_op jit(solution)/shard_map/ppermute | solution.py:201
  17.2 0.2 collective-permute-start.6
  17.4 0.7 %copy-done.2 = f32[8]{0:T(128)S(1)} copy-done((f32[8]{0:T(128)S(1)}, f32[8]{0:T(128)}, u32[]{:S(2)}) %copy-start.2) | copy-done | bytes 56
  18.1 0.0 copy-done.3
  18.1 0.3 denominator.1
  18.3 0.3 kept.1
  18.6 0.0 collective-permute-done.4
  18.6 2.5 %collective-permute-done.5 = bf16[2,128,128]{2,1,0:T(8,128)(2,1)S(1)} collective-permute-done((bf16[2,128,128]{2,1,0:T(8,128)(2,1)S(1)}, bf16[2,128,128]{2,1,0:T(8,128)(2,1)S(1)}, u32[]{:S(2)}, u32[]{:S(2)}) %collective-permute-start.5) | collective-permute-done | bytes 65568 | tf_op jit(solution)/shard_map/ppermute | solution.py:201
  21.2 2.1 %collective-permute-done.6 = bf16[2,128,128]{2,1,0:T(8,128)(2,1)S(1)} collective-permute-done((bf16[2,128,128]{2,1,0:T(8,128)(2,1)S(1)}, bf16[2,128,128]{2,1,0:T(8,128)(2,1)S(1)}, u32[]{:S(2)}, u32[]{:S(2)}) %collective-permute-start.6) | collective-permute-done | bytes 65568 | tf_op jit(solution)/shard_map/ppermute | solution.py:201
  23.2 0.1 divide_convert_fusion.refs_0_
  23.3 0.1 collective-permute-start.7
  23.4 1.4 %collective-permute-start.8 = (bf16[2,128,128]{2,1,0:T(8,128)(2,1)S(1)}, bf16[2,128,128]{2,1,0:T(8,128)(2,1)S(1)}, u32[]{:S(2)}, u32[]{:S(2)}) collective-permute-start(bf16[2,128,128]{2,1,0:T(8,128)(2,1)S(1)} %divide_convert_fusion.refs_0_), channel_id=1, source_target_pairs={{0,2},{1,3},{2,0},{3,1},{4,6},{5,7},{6,4},{7,5},{8,10},{9,11},{10,... | collective-permute-start | bytes 196616 | tf_op jit(solution)/shard_map/ppermute | solution.py:201
  24.7 2.6 %collective-permute-start.9 = (bf16[2,128,128]{2,1,0:T(8,128)(2,1)S(1)}, bf16[2,128,128]{2,1,0:T(8,128)(2,1)S(1)}, u32[]{:S(2)}, u32[]{:S(2)}) collective-permute-start(bf16[2,128,128]{2,1,0:T(8,128)(2,1)S(1)} %divide_convert_fusion.refs_0_), channel_id=1, source_target_pairs={{0,3},{1,0},{2,1},{3,2},{4,7},{5,4},{6,5},{7,6},{8,11},{9,8},{10,9... | collective-permute-start | bytes 196616 | tf_op jit(solution)/shard_map/ppermute | solution.py:201
  27.3 2.1 %collective-permute-done.7.refs_1_ = bf16[2,128,128]{2,1,0:T(8,128)(2,1)S(1)} collective-permute-done((bf16[2,128,128]{2,1,0:T(8,128)(2,1)S(1)}, bf16[2,128,128]{2,1,0:T(8,128)(2,1)S(1)}, u32[]{:S(2)}, u32[]{:S(2)}) %collective-permute-start.7) | collective-permute-done | bytes 65568 | tf_op jit(solution)/shard_map/ppermute | solution.py:201
  29.4 0.7 %collective-permute-done.9.refs_3_ = bf16[2,128,128]{2,1,0:T(8,128)(2,1)S(1)} collective-permute-done((bf16[2,128,128]{2,1,0:T(8,128)(2,1)S(1)}, bf16[2,128,128]{2,1,0:T(8,128)(2,1)S(1)}, u32[]{:S(2)}, u32[]{:S(2)}) %collective-permute-start.9) | collective-permute-done | bytes 65568 | tf_op jit(solution)/shard_map/ppermute | solution.py:201
  30.1 0.7 %join.1 = bf16[8,128,128]{2,1,0:T(8,128)(2,1)} custom-call(bf16[2,128,128]{2,1,0:T(8,128)(2,1)S(1)} %divide_convert_fusion.refs_0_, bf16[2,128,128]{2,1,0:T(8,128)(2,1)S(1)} %collective-permute-done.7.refs_1_, bf16[2,128,128]{2,1,0:T(8,128)(2,1)S(1)} %collective-permute-done.8.refs_2_, bf16[2,128,128]{2,1,0:T(8,128)(2,1)S(1)} %collective-permute-done.9.refs_3_), custom_call_target="tpu_custom_call" | custom-call | tf_op jit(solution)/shard_map/join/pallas_call | solution.py:210
  (10 shorter events, 0.1 us)
Async XLA Ops:
  0.0 0.7 %copy-start.1 = (s32[8]{0:T(128)S(1)}, s32[8]{0:T(128)}, u32[]{:S(2)}) copy-start(s32[8]{0:T(128)} %param.9) | copy-start | bytes 100
  0.0 1.9 %collective-permute-start = (bf16[8,128,128]{2,1,0:T(8,128)(2,1)}, bf16[8,128,128]{2,1,0:T(8,128)(2,1)S(1)}, u32[]{:S(2)}, u32[]{:S(2)}) collective-permute-start(bf16[8,128,128]{2,1,0:T(8,128)(2,1)} %bitcast.17), channel_id=1, source_target_pairs={{0,4},{4,0},{8,12},{12,8},{16,20},{20,16},{24,28},{28,24},{1,5},{5... | collective-permute-start | bytes 786440 | tf_op jit(solution)/shard_map/ppermute | solution.py:126
  0.7 0.9 %copy-start = (bf16[1,8,128,128]{3,2,1,0:T(8,128)(2,1)S(1)}, bf16[1,8,128,128]{3,2,1,0:T(8,128)(2,1)}, u32[]{:S(2)}) copy-start(bf16[1,8,128,128]{3,2,1,0:T(8,128)(2,1)} %param.6) | copy-start | bytes 786436
  1.9 0.7 %copy-start.4 = (s32[4,8]{1,0:T(4,128)S(1)}, s32[4,8]{1,0:T(4,128)}, u32[]{:S(2)}) copy-start(s32[4,8]{1,0:T(4,128)} %param.8) | copy-start | bytes 388
  2.6 6.1 %collective-permute-start.1 = (bf16[2,128,128]{2,1,0:T(8,128)(2,1)S(1)}, bf16[2,128,128]{2,1,0:T(8,128)(2,1)S(1)}, u32[]{:S(2)}, u32[]{:S(2)}) collective-permute-start(bf16[2,128,128]{2,1,0:T(8,128)(2,1)S(1)} %get-tuple-element.30), channel_id=1, source_target_pairs={{0,8},{4,12},{8,0},{12,4},{16,24},{20,28},{24,16},{28,20},{1,9},{5... | collective-permute-start | bytes 196616 | tf_op jit(solution)/shard_map/ppermute | solution.py:151
  5.4 4.3 %collective-permute-start.2 = (bf16[2,128,128]{2,1,0:T(8,128)(2,1)S(1)}, bf16[2,128,128]{2,1,0:T(8,128)(2,1)S(1)}, u32[]{:S(2)}, u32[]{:S(2)}) collective-permute-start(bf16[2,128,128]{2,1,0:T(8,128)(2,1)S(1)} %get-tuple-element.31), channel_id=1, source_target_pairs={{0,16},{4,20},{8,24},{12,28},{16,0},{20,4},{24,8},{28,12},{1,17},{... | collective-permute-start | bytes 196616 | tf_op jit(solution)/shard_map/ppermute | solution.py:151
  6.9 5.2 %collective-permute-start.3 = (bf16[2,128,128]{2,1,0:T(8,128)(2,1)S(1)}, bf16[2,128,128]{2,1,0:T(8,128)(2,1)S(1)}, u32[]{:S(2)}, u32[]{:S(2)}) collective-permute-start(bf16[2,128,128]{2,1,0:T(8,128)(2,1)S(1)} %get-tuple-element.32), channel_id=1, source_target_pairs={{0,24},{4,28},{8,16},{12,20},{16,8},{20,12},{24,0},{28,4},{1,25},{... | collective-permute-start | bytes 196616 | tf_op jit(solution)/shard_map/ppermute | solution.py:151
  12.9 5.7 %collective-permute-start.4 = (bf16[2,128,128]{2,1,0:T(8,128)(2,1)S(1)}, bf16[2,128,128]{2,1,0:T(8,128)(2,1)S(1)}, u32[]{:S(2)}, u32[]{:S(2)}) collective-permute-start(bf16[2,128,128]{2,1,0:T(8,128)(2,1)S(1)} %get-tuple-element.34), channel_id=1, source_target_pairs={{0,1},{1,0},{2,3},{3,2},{4,5},{5,4},{6,7},{7,6},{8,9},{9,8},{10,11... | collective-permute-start | bytes 196616 | tf_op jit(solution)/shard_map/ppermute | solution.py:201
  14.6 6.6 %collective-permute-start.5 = (bf16[2,128,128]{2,1,0:T(8,128)(2,1)S(1)}, bf16[2,128,128]{2,1,0:T(8,128)(2,1)S(1)}, u32[]{:S(2)}, u32[]{:S(2)}) collective-permute-start(bf16[2,128,128]{2,1,0:T(8,128)(2,1)S(1)} %get-tuple-element.35), channel_id=1, source_target_pairs={{0,2},{1,3},{2,0},{3,1},{4,6},{5,7},{6,4},{7,5},{8,10},{9,11},{10,... | collective-permute-start | bytes 196616 | tf_op jit(solution)/shard_map/ppermute | solution.py:201
  17.2 6.1 %collective-permute-start.6 = (bf16[2,128,128]{2,1,0:T(8,128)(2,1)S(1)}, bf16[2,128,128]{2,1,0:T(8,128)(2,1)S(1)}, u32[]{:S(2)}, u32[]{:S(2)}) collective-permute-start(bf16[2,128,128]{2,1,0:T(8,128)(2,1)S(1)} %get-tuple-element.36), channel_id=1, source_target_pairs={{0,3},{1,2},{2,1},{3,0},{4,7},{5,6},{6,5},{7,4},{8,11},{9,10},{10,... | collective-permute-start | bytes 196616 | tf_op jit(solution)/shard_map/ppermute | solution.py:201
  17.4 0.7 %copy-start.2 = (f32[8]{0:T(128)S(1)}, f32[8]{0:T(128)}, u32[]{:S(2)}) copy-start(f32[8]{0:T(128)} %param.10) | copy-start | bytes 100
  17.4 0.7 %copy-start.3 = (f32[128]{0:T(128)S(1)}, f32[128]{0:T(128)}, u32[]{:S(2)}) copy-start(f32[128]{0:T(128)} %param.11) | copy-start | bytes 1540
  23.3 6.1 %collective-permute-start.7 = (bf16[2,128,128]{2,1,0:T(8,128)(2,1)S(1)}, bf16[2,128,128]{2,1,0:T(8,128)(2,1)S(1)}, u32[]{:S(2)}, u32[]{:S(2)}) collective-permute-start(bf16[2,128,128]{2,1,0:T(8,128)(2,1)S(1)} %divide_convert_fusion.refs_0_), channel_id=1, source_target_pairs={{0,1},{1,2},{2,3},{3,0},{4,5},{5,6},{6,7},{7,4},{8,9},{9,10},{10,1... | collective-permute-start | bytes 196616 | tf_op jit(solution)/shard_map/ppermute | solution.py:201
  23.4 6.1 %collective-permute-start.8 = (bf16[2,128,128]{2,1,0:T(8,128)(2,1)S(1)}, bf16[2,128,128]{2,1,0:T(8,128)(2,1)S(1)}, u32[]{:S(2)}, u32[]{:S(2)}) collective-permute-start(bf16[2,128,128]{2,1,0:T(8,128)(2,1)S(1)} %divide_convert_fusion.refs_0_), channel_id=1, source_target_pairs={{0,2},{1,3},{2,0},{3,1},{4,6},{5,7},{6,4},{7,5},{8,10},{9,11},{10,... | collective-permute-start | bytes 196616 | tf_op jit(solution)/shard_map/ppermute | solution.py:201
  24.7 5.4 %collective-permute-start.9 = (bf16[2,128,128]{2,1,0:T(8,128)(2,1)S(1)}, bf16[2,128,128]{2,1,0:T(8,128)(2,1)S(1)}, u32[]{:S(2)}, u32[]{:S(2)}) collective-permute-start(bf16[2,128,128]{2,1,0:T(8,128)(2,1)S(1)} %divide_convert_fusion.refs_0_), channel_id=1, source_target_pairs={{0,3},{1,0},{2,1},{3,2},{4,7},{5,4},{6,5},{7,6},{8,11},{9,8},{10,9... | collective-permute-start | bytes 196616 | tf_op jit(solution)/shard_map/ppermute | solution.py:201
